TPU v7x, 32 devices: a whole 2x2x4 slice. The times are simulated.
32 devices in a mesh: dp: 4 (over z), rows: 8 (over y, x, core).
Axes of the slice: x: 2, y: 2, z: 4, core: 2. Of those that a mesh axis runs over, the one named last changes fastest.
Arguments:
- inputs: bfloat16 [2, 8192, 9216], P(None, 'dp', 'rows'), may hold values from -21 to 21
- weights: bfloat16 [2, 9216, 4096], P(None, 'rows'), may hold values from -0.0625 to 0.0625
- bias: float32 [2, 4096], P(None, 'rows'), may hold values from -3 to 3
- stitch: float32 [2, 2, 4096], P(None, None, 'rows'), may hold values from 0.2 to 1
- cotangent: bfloat16 [2, 4096, 8192], P(None, 'rows', 'dp'), may hold values from -6 to 6
- valid: int32 [8192], P('dp'), may hold values from 0 to 1, as said below
- size_class: int32 [8192], P('dp'), may hold values from 195 to 227, as said below
Outputs:
- stitched: bfloat16 [2, 4096, 8192], P(None, 'rows', 'dp')
- grad_inputs: bfloat16 [2, 8192, 9216], P(None, 'dp', 'rows')
- grad_weights: float32 [2, 9216, 4096], P(None, 'rows', 'dp')
- grad_bias: float32 [2, 4096], P(None, 'rows')
- grad_stitch: float32 [2, 2, 4096], P(None, None, 'rows')
- rms_values: float32 [3], replicated
Inputs may be any that keep to these rules, and one draw needn't show every extreme that they name: The first image of every aligned block of 2048 images is valid. `size_class`: each entry is 227 or 195.
All inputs are finite; a program needn't handle non-finite values.
Results may differ from a plain program's by a relative error of at most 0.006.
Values may be sent and summed in bfloat16 or wider, within the bound.
A program may use at most 256 MiB of HBM per device.

v0:
```python
import jax
import jax.numpy as jnp
from jax import lax
from jax.sharding import PartitionSpec as P

F = 9216
C = 4096


def per_device(inputs, weights, bias, stitch, cotangent, valid, size_class):
    width = inputs.shape[2]
    place = lax.iota(jnp.int32, width) % 36
    padded = (place // 6 == 5) | (place % 6 == 5)
    keep = jnp.where((size_class == 195)[:, None] & padded[None, :], 1.0, 1.0) * jnp.where(
        (size_class == 195)[:, None] & padded[None, :], 0.0, 1.0
    )
    keep = keep.astype(jnp.bfloat16)
    used = inputs * keep[None]
    part = weights
    linear = jnp.transpose(
        lax.psum_scatter(
            jnp.einsum("tfc,tbf->ctb", part, used, preferred_element_type=jnp.float32),
            "rows",
            scatter_dimension=0,
            tiled=True,
        ),
        (1, 0, 2),
    )
    pre = linear + bias[:, :, None]
    act = jax.nn.relu(pre)
    out = jnp.sum(stitch[:, :, :, None] * act[None], axis=1)
    stitched = out.astype(jnp.bfloat16)
    weight_valid = valid.astype(jnp.float32)
    upstream = cotangent.astype(jnp.float32) * weight_valid[None, None, :]
    grad_act = jnp.sum(stitch[:, :, :, None] * upstream[:, None], axis=0)
    grad_pre = jnp.where(pre > 0, grad_act, 0.0).astype(jnp.bfloat16)
    grad_bias = jnp.sum(grad_pre.astype(jnp.float32), axis=2)
    grad_stitch = jnp.sum(upstream[:, None] * act[None], axis=3)
    piece = lax.all_gather(grad_pre, "rows", axis=1, tiled=True)
    part = weights
    total_x = jnp.einsum("tcb,tfc->tbf", piece, part, preferred_element_type=jnp.float32)
    block = jnp.einsum("tbf,tcb->tfc", used, piece, preferred_element_type=jnp.float32)
    total_w = block
    total_x, total_w = (total_x, total_w)
    grad_inputs = (total_x * keep.astype(jnp.float32)[None]).astype(jnp.bfloat16)
    grad_weights = lax.psum_scatter(total_w, "dp", scatter_dimension=2, tiled=True)
    used_wide = used.astype(jnp.float32)
    partial_value = jnp.stack(
        [
            jnp.sum(weight_valid[None, :, None] * used_wide * used_wide),
            jnp.sum(weight_valid[None, None, :] * pre * pre),
            jnp.sum(weight_valid[None, None, :] * out * out),
            jnp.sum(weight_valid),
        ]
    )
    grad_bias, grad_stitch = lax.psum((grad_bias, grad_stitch), "dp")
    totals = lax.psum(partial_value, ("dp", "rows"))
    count = totals[3] / lax.axis_size("rows")
    rms_values = jnp.sqrt(
        jnp.stack(
            [totals[0] / (count * 2 * F), totals[1] / (count * 2 * C), totals[2] / (count * 2 * C)]
        )
    )
    return (stitched, grad_inputs, grad_weights, grad_bias, grad_stitch, rms_values)


def solution(mesh):
    in_specs = (
        P(None, "dp", "rows"),
        P(None, "rows", None),
        P(None, "rows"),
        P(None, None, "rows"),
        P(None, "rows", "dp"),
        P("dp"),
        P("dp"),
    )
    out_specs = (
        P(None, "rows", "dp"),
        P(None, "dp", "rows"),
        P(None, "rows", "dp"),
        P(None, "rows"),
        P(None, None, "rows"),
        P(),
    )
    return jax.shard_map(
        per_device, mesh=mesh, in_specs=in_specs, out_specs=out_specs, check_vma=False
    )
```

profile of v0, /device:TPU:8, one launch (start us, length us, event | category | flops | bytes accessed | tf_op | source)
XLA Modules:
  0.0 1350.3 jit_solution(14084836834805063810)
XLA Ops:
  7.2 0.7 broadcast_compare_fusion
  7.9 4.2 fusion.9
  12.2 2.2 copy-done
  14.4 53.8 %convolution_bitcast_fusion = f32[4096,2,2048]{0,2,1:T(8,128)} fusion(bf16[2,1152,4096]{2,1,0:T(8,128)(2,1)} %param.8, bf16[2,2048,1152]{2,1,0:T(8,128)(2,1)} %param.7, bf16[2048,1152]{1,0:T(8,128)(2,1)S(1)} %get-tuple-element.24), kind=kOutput, calls=%fused_computation.1 | convolution fusion | flops 38659424256 | bytes 100139008 | tf_op jit(solution)/shard_map/tfc,tbf->ctb/dot_general | solution.py:22
  68.5 6.2 copy.20
  74.7 7.8 convert_multiply_fusion
  82.5 9.4 copy.21
  91.9 361.4 %reduce-scatter.3.cloned.1.call-done = f32[512,2,2048]{0,2,1:T(8,128)} async-done(((f32[4096,2,2048]{0,2,1:T(8,128)}), f32[512,2,2048]{0,2,1:T(8,128)}) %reduce-scatter.3.cloned.1.call-update) | async-done | bytes 8388624 | tf_op jit(solution)/shard_map/reduce_scatter | solution.py:21
  453.3 8.2 fusion.3
  461.5 8.7 copy.19
  470.3 14.0 %multiply_reduce_fusion = (f32[2,2,512]{2,1,0:T(2,128)S(1)}, f32[2,512,2048]{2,1,0:T(8,128)}, bf16[2,512,2048]{2,1,0:T(8,128)(2,1)}) fusion(f32[2,512,2048]{2,1,0:T(8,128)} %copy.21, f32[2,512,2048]{2,1,0:T(8,128)} %copy.19, f32[2,2,512]{2,1,0:T(2,128)S(1)} %copy-done.3), kind=kLoop, calls=%fused_computation.4 | loop fusion | flops 20969472 | bytes 29376512 | tf_op jit(solution)/shard_map/reduce_sum | solution.py:38
  484.2 8.7 copy.25
  492.9 6.2 copy.22
  499.1 11.0 fusion.1
  510.4 167.3 %all-gather.2.cloned.1.call-done = bf16[2,4096,2048]{1,2,0:T(8,128)(2,1)} async-done(((bf16[2,512,2048]{1,2,0:T(8,128)(2,1)}), bf16[2,4096,2048]{1,2,0:T(8,128)(2,1)}) %all-gather.2.cloned.1.call-update) | async-done | bytes 33554448 | tf_op jit(solution)/shard_map/all_gather | solution.py:39
  677.7 48.4 %fusion.4 = f32[2,1152,4096]{2,1,0:T(8,128)} fusion(bf16[2,4096,2048]{1,2,0:T(8,128)(2,1)} %all-gather.2.cloned.1.call-done, bf16[2,2048,1152]{2,1,0:T(8,128)(2,1)} %param.7, bf16[2048,1152]{1,0:T(8,128)(2,1)} %copy-done), kind=kOutput, calls=%fused_computation.17 | convolution fusion | flops 38659424256 | bytes 85458944 | tf_op jit(solution)/shard_map/tbf,tcb->tfc/dot_general | solution.py:42
  726.1 0.6 convert_reduce_fusion.1
  726.7 10.5 fusion
  737.2 2.7 pad_maximum_fusion
  739.9 43.4 %psum.23 = f32[4]{0:T(128)S(1)} all-reduce(f32[4]{0:T(128)S(1)} %pad_maximum_fusion), channel_id=1, replica_groups=mesh['dp'=4,'rows'=8] {'dp','rows'}, use_global_device_ids=true, to_apply=%region_12.13 | all-reduce | flops 4 | bytes 32 | tf_op jit(solution)/shard_map/psum | solution.py:57
  783.3 6.2 convert_element_type.39
  793.3 20.4 %all-reduce = (f32[2,512]{1,0:T(2,128)}, f32[2,2,512]{2,1,0:T(2,128)}) all-reduce(f32[2,512]{1,0:T(2,128)S(1)} %get-tuple-element.21, f32[2,2,512]{2,1,0:T(2,128)S(1)} %get-tuple-element.12), channel_id=1, replica_groups=mesh['dp'=4,'rows'=8] {'dp'}, use_global_device_ids=true, to_apply=%region_5.6 | all-reduce | flops 3072 | bytes 24576 | tf_op jit(solution)/shard_map/psum | solution.py:56
  814.3 52.0 %multiply_convert_fusion = bf16[2,2048,1152]{2,1,0:T(8,128)(2,1)} fusion(bf16[2,4096,2048]{1,2,0:T(8,128)(2,1)} %all-gather.2.cloned.1.call-done, bf16[2,1152,4096]{2,1,0:T(8,128)(2,1)} %param.8, f32[2048,1152]{1,0:T(8,128)} %get-tuple-element.23), kind=kOutput, calls=%fused_computation.3 | convolution fusion | flops 38664142848 | bytes 71303168 | tf_op jit(solution)/shard_map/tcb,tfc->tbf/dot_general | solution.py:41
  866.4 477.4 %reduce-scatter.5.cloned.1.call-done = f32[2,1152,1024]{2,1,0:T(8,128)} async-done(((f32[2,1152,4096]{2,1,0:T(8,128)}), f32[2,1152,1024]{2,1,0:T(8,128)}) %reduce-scatter.5.cloned.1.call-update) | async-done | bytes 9437200 | tf_op jit(solution)/shard_map/reduce_scatter | solution.py:46
  (17 shorter events, 1.8 us)
Async XLA Ops:
  7.2 446.1 %reduce-scatter.3.cloned.1.call-start = ((), (), s32[]{:S(2)}) async-start(), calls=%async_computation.2 | async-start | bytes 75497472 | tf_op jit(solution)/shard_map/reduce_scatter | solution.py:21
  12.2 2.2 copy-start
  68.2 6.5 copy-start.1
  68.2 609.5 %all-gather.2.cloned.1.call-start = ((), (), s32[]{:S(2)}) async-start(), calls=%async_computation.3 | async-start | bytes 37748736 | tf_op jit(solution)/shard_map/all_gather | solution.py:39
  82.5 370.8 %copy-start.2 = (f32[2,512]{1,0:T(2,128)S(1)}, f32[2,512]{1,0:T(2,128)}, u32[]{:S(2)}) copy-start(f32[2,512]{1,0:T(2,128)} %param.9) | copy-start | bytes 12292
  461.5 8.7 copy-start.3
  510.1 833.6 %reduce-scatter.5.cloned.1.call-start = ((), (), s32[]{:S(2)}) async-start(), calls=%async_computation.4 | async-start | bytes 47185920 | tf_op jit(solution)/shard_map/reduce_scatter | solution.py:46
Sparse Core Ops, SparseCore 0:
  68.4 384.9 reduce-scatter.2
  510.2 167.4 all-gather.1
  726.2 617.5 reduce-scatter.4
where the time goes:
time: 1360 us; the launch traced here: 1350 us
  waiting for transfers between devices  1010 us (74%)
  matrix products  154 us (11%)
  other arithmetic  66.5 us (5%)
  blocking collectives  63.8 us (5%)
  local copies, waits for them, and re-layouts  42.1 us (3%)
  between operations  17 us (1%)
    reduce_scatter x1, waiting for transfers between devices, per_device(): lax.psum_scatter(total_w, 'dp', scatter_dimension=2, tiled=True)  477 us
    reduce_scatter x1, waiting for transfers between devices, per_device(): lax.psum_scatter(jnp.einsum('tfc,tbf->ctb', part, used, preferred_element...  361 us
    all_gather x1, waiting for transfers between devices, per_device(): piece = lax.all_gather(grad_pre, 'rows', axis=1, tiled=True)  167 us
    dot_general x1, matrix products, per_device(): jnp.einsum('tfc,tbf->ctb', part, used, preferred_element_type=jnp.float32)  53.8 us
    dot_general x1, matrix products, per_device(): jnp.einsum('tcb,tfc->tbf', piece, part, preferred_element_type=jnp.float32)  52 us
    dot_general x1, matrix products, per_device(): jnp.einsum('tbf,tcb->tfc', used, piece, preferred_element_type=jnp.float32)  48.4 us
    psum x1, blocking collectives, per_device(): totals = lax.psum(partial_value, ('dp', 'rows'))  43.4 us
  transfers between devices with their start and end apart: 3, of which 3 were waited for; matrix products, arithmetic and copies ran while one was open for 7% of the time, Pallas kernels for 0%

commit v1 on v0

v1 whole, which is shorter than its diff:
```python
import jax
import jax.numpy as jnp
from jax import lax
from jax.sharding import PartitionSpec as P

F = 9216
C = 4096
BLOCK = 128


def chain(own, up):
    size = lax.axis_size("dp")
    here = lax.axis_index("dp")
    got = None
    for step in range(size - 1):
        dest = size - 1 - step + here if up else step - (size - 1) + here
        dest = jnp.clip(dest, 0, size - 1)
        term = lax.dynamic_index_in_dim(own, dest, 0, keepdims=False)
        if got is not None:
            term = (term.astype(jnp.float32) + got.astype(jnp.float32)).astype(jnp.bfloat16)
        pairs = [(z, z + 1) for z in range(step + 1)]
        if not up:
            pairs = [(size - 1 - a, size - 1 - b) for a, b in pairs]
        got = lax.ppermute(term, "dp", pairs)
    return got


def per_device(inputs, weights, bias, stitch, cotangent, valid, size_class):
    rows = lax.axis_size("rows")
    size = lax.axis_size("dp")
    here = lax.axis_index("dp")
    width = inputs.shape[2]
    mine = bias.shape[1]
    step = min(BLOCK, mine)
    blocks = mine // step
    place = lax.iota(jnp.int32, width) % 36
    padded = (place // 6 == 5) | (place % 6 == 5)
    dropped = (size_class == 195)[:, None] & padded[None, :]
    used = jnp.where(dropped[None], jnp.zeros((), jnp.bfloat16), inputs)
    split = weights.reshape(2, width, rows, mine)
    weight_valid = valid.astype(jnp.float32)
    pieces, stitched, grad_bias, grad_stitch, square_pre, square_out = [], [], [], [], [], []
    grad_weights = []
    mats = [split[:, :, :, k * step : (k + 1) * step] for k in range(blocks)]
    sums = []
    for k in range(blocks):
        part = jnp.einsum("tfrc,tbf->rctb", mats[k], used, preferred_element_type=jnp.float32)
        sums.append(
            lax.psum_scatter(part.reshape(rows * step, 2, -1), "rows", scatter_dimension=0, tiled=True)
        )
    for k in range(blocks):
        cut = slice(k * step, (k + 1) * step)
        pre = jnp.transpose(sums[k], (1, 0, 2)) + bias[:, cut, None]
        act = jax.nn.relu(pre)
        mix = stitch[:, :, cut, None]
        out = jnp.sum(mix * act[None], axis=1)
        stitched.append(out.astype(jnp.bfloat16))
        upstream = cotangent[:, cut].astype(jnp.float32) * weight_valid[None, None, :]
        grad_act = jnp.sum(mix * upstream[:, None], axis=0)
        grad_pre = jnp.where(pre > 0, grad_act, 0.0).astype(jnp.bfloat16)
        grad_bias.append(jnp.sum(grad_pre.astype(jnp.float32), axis=2))
        grad_stitch.append(jnp.sum(upstream[:, None] * act[None], axis=3))
        square_pre.append(jnp.sum(weight_valid[None, None, :] * pre * pre))
        square_out.append(jnp.sum(weight_valid[None, None, :] * out * out))
        piece = lax.all_gather(grad_pre, "rows", axis=0)
        pieces.append(piece)
        block = jnp.einsum("tbf,rtcb->rtfc", used, piece, preferred_element_type=jnp.float32)
        block = block.reshape(size, rows // size, 2, width, step)
        own = block.astype(jnp.bfloat16)
        total = lax.dynamic_index_in_dim(block, here, 0, keepdims=False)
        total = total + chain(own, True).astype(jnp.float32) + chain(own, False).astype(jnp.float32)
        grad_weights.append(total)
    total_x = sum(
        jnp.einsum("rtcb,tfrc->tbf", pieces[k], mats[k], preferred_element_type=jnp.float32)
        for k in range(blocks)
    )
    grad_inputs = jnp.where(dropped[None], 0.0, total_x).astype(jnp.bfloat16)
    grad_weights = jnp.stack(grad_weights, axis=0)
    grad_weights = jnp.transpose(grad_weights, (2, 3, 1, 0, 4)).reshape(2, width, -1)
    stitched = jnp.concatenate(stitched, axis=1)
    grad_bias = jnp.concatenate(grad_bias, axis=1)
    grad_stitch = jnp.concatenate(grad_stitch, axis=2)
    used_wide = used.astype(jnp.float32)
    partial_value = jnp.stack(
        [
            jnp.sum(weight_valid[None, :, None] * used_wide * used_wide),
            sum(square_pre),
            sum(square_out),
            jnp.sum(weight_valid),
        ]
    )
    grad_bias, grad_stitch = lax.psum((grad_bias, grad_stitch), "dp")
    totals = lax.psum(partial_value, ("dp", "rows"))
    count = totals[3] / rows
    rms_values = jnp.sqrt(
        jnp.stack(
            [totals[0] / (count * 2 * F), totals[1] / (count * 2 * C), totals[2] / (count * 2 * C)]
        )
    )
    return (stitched, grad_inputs, grad_weights, grad_bias, grad_stitch, rms_values)


def solution(mesh):
    in_specs = (
        P(None, "dp", "rows"),
        P(None, "rows", None),
        P(None, "rows"),
        P(None, None, "rows"),
        P(None, "rows", "dp"),
        P("dp"),
        P("dp"),
    )
    out_specs = (
        P(None, "rows", "dp"),
        P(None, "dp", "rows"),
        P(None, "rows", "dp"),
        P(None, "rows"),
        P(None, None, "rows"),
        P(),
    )
    return jax.shard_map(
        per_device, mesh=mesh, in_specs=in_specs, out_specs=out_specs, check_vma=False
    )
```

time: 1360 us -> 1190 us (0.88)
  waiting for transfers between devices: 1010 us -> 659 us
  matrix products: 154 us -> 233 us
  starting transfers between devices: 0.52 us -> 47.3 us
  local copies, waits for them, and re-layouts: 42.1 us -> 83.2 us
  other arithmetic: 66.5 us -> 80.9 us
    reduce_scatter x2 -> x4, waiting for transfers between devices: 839 us -> 402 us  [per_device(): lax.psum_scatter(part.reshape(rows * step, 2, -1), 'rows', scatter_dimens...]
    ppermute x0 -> x24, waiting for transfers between devices: none -> 225 us  [chain(): got = lax.ppermute(term, 'dp', pairs)]
    all_gather x1 -> x4, waiting for transfers between devices: 167 us -> 30.9 us  [per_device(): piece = lax.all_gather(grad_pre, 'rows', axis=0)]
    unnamed x0 -> x4, matrix products: none -> 76.4 us
    ppermute x0 -> x24, starting transfers between devices: none -> 46 us  [chain(): got = lax.ppermute(term, 'dp', pairs)]
    unnamed x9 -> x55, local copies, waits for them, and re-layouts: 8.46 us -> 31.3 us
    convert_element_type x2 -> x13, other arithmetic: 10.4 us -> 29.1 us  [the longest x12 24.7 us: chain(): (term.astype(jnp.float32) + got.astype(jnp.float32)).astype(jnp.bfloat16)]
    reduce_sum x2 -> x0, local copies, waits for them, and re-layouts: 14.9 us -> none  [the longest x1 8.67 us: per_device(): out = jnp.sum(stitch[:, :, :, None] * act[None], axis=1)]
  transfers between devices with their start and end apart: 3 -> 32, of which waited for: 3 -> 17; matrix products, arithmetic and copies ran while one was open for 7% -> 25% of each run, Pallas kernels for 0% -> 0%
where the time goes in v1:
time: 1190 us; the launch traced here: 1180 us
  waiting for transfers between devices  659 us (55%)
  matrix products  233 us (20%)
  local copies, waits for them, and re-layouts  83.2 us (7%)
  other arithmetic  80.9 us (7%)
  blocking collectives  54.3 us (5%)
  starting transfers between devices  47.3 us (4%)
  between operations  23.6 us (2%)
    reduce_scatter x4, waiting for transfers between devices, per_device(): lax.psum_scatter(part.reshape(rows * step, 2, -1), 'rows', scatter_dimens...  402 us
    ppermute x24, waiting for transfers between devices, chain(): got = lax.ppermute(term, 'dp', pairs)  225 us
    dot_general x4, matrix products, per_device(): jnp.einsum('rtcb,tfrc->tbf', pieces[k], mats[k], preferred_element_type=j...  82.3 us
    unnamed x4, matrix products  76.4 us
    dot_general x4, matrix products, per_device(): jnp.einsum('tbf,rtcb->rtfc', used, piece, preferred_element_type=jnp.floa...  74.7 us
    ppermute x24, starting transfers between devices, chain(): got = lax.ppermute(term, 'dp', pairs)  46 us
    psum x1, blocking collectives, per_device(): totals = lax.psum(partial_value, ('dp', 'rows'))  39.5 us
    unnamed x55, local copies, waits for them, and re-layouts  31.3 us
  transfers between devices with their start and end apart: 32, of which 17 were waited for; matrix products, arithmetic and copies ran while one was open for 25% of the time, Pallas kernels for 0%

profile of v1, /device:TPU:8, one launch (start us, length us, event | category | flops | bytes accessed | tf_op | source)
XLA Modules:
  0.0 1182.3 jit_solution(11360257432043115924)
XLA Ops:
  7.9 24.6 %copy.69 = bf16[2,1152,4096]{1,2,0:T(8,128)(2,1)} copy(bf16[2,1152,4096]{2,1,0:T(8,128)(2,1)} %param.8) | data formatting | bytes 37748736 | tf_op args[1]
  66.7 19.6 %convolution_bitcast_fusion = f32[1024,2,2048]{2,0,1:T(8,128)} fusion(bf16[2,1152,1024]{1,2,0:T(8,128)(2,1)} %bitcast.246, bf16[2,2048,1152]{2,1,0:T(8,128)(2,1)} %param.7, pred[2048,1152]{1,0:T(8,128)(4,1)S(1)} %broadcast_and_fusion), kind=kOutput, calls=%fused_computation.24 | convolution fusion | flops 9668395008 | bytes 33292288
  86.9 20.1 %convolution_bitcast_fusion.2 = f32[1024,2,2048]{2,0,1:T(8,128)} fusion(bf16[2,1152,1024]{1,2,0:T(8,128)(2,1)} %bitcast.248, bf16[2,2048,1152]{2,1,0:T(8,128)(2,1)} %param.7, pred[2048,1152]{1,0:T(8,128)(4,1)S(1)} %broadcast_and_fusion), kind=kOutput, calls=%fused_computation.26 | convolution fusion | flops 9668395008 | bytes 33292288
  132.4 51.5 %reduce-scatter.9.cloned.1.call-done = f32[128,2,2048]{2,0,1:T(8,128)} async-done(((f32[1024,2,2048]{2,0,1:T(8,128)}), f32[128,2,2048]{2,0,1:T(8,128)}) %reduce-scatter.9.cloned.1.call-update) | async-done | bytes 2097168 | tf_op jit(solution)/shard_map/reduce_scatter | solution.py:49
  183.9 119.5 %reduce-scatter.11.cloned.1.call-done = f32[128,2,2048]{2,0,1:T(8,128)} async-done(((f32[1024,2,2048]{2,0,1:T(8,128)}), f32[128,2,2048]{2,0,1:T(8,128)}) %reduce-scatter.11.cloned.1.call-update) | async-done | bytes 2097168 | tf_op jit(solution)/shard_map/reduce_scatter | solution.py:49
  311.8 111.2 %reduce-scatter.7.cloned.1.call-done = f32[128,2,2048]{2,0,1:T(8,128)} async-done(((f32[1024,2,2048]{2,0,1:T(8,128)}), f32[128,2,2048]{2,0,1:T(8,128)}) %reduce-scatter.7.cloned.1.call-update) | async-done | bytes 2097168 | tf_op jit(solution)/shard_map/reduce_scatter | solution.py:49
  423.0 119.4 %reduce-scatter.5.cloned.1.call-done = f32[128,2,2048]{2,0,1:T(8,128)} async-done(((f32[1024,2,2048]{2,0,1:T(8,128)}), f32[128,2,2048]{2,0,1:T(8,128)}) %reduce-scatter.5.cloned.1.call-update) | async-done | bytes 2097168 | tf_op jit(solution)/shard_map/reduce_scatter | solution.py:49
  575.0 39.5 %psum.23 = f32[4]{0:T(128)S(1)} all-reduce(f32[4]{0:T(128)S(1)} %pad_maximum_fusion.3), channel_id=1, replica_groups=mesh['dp'=4,'rows'=8] {'dp','rows'}, use_global_device_ids=true, to_apply=%region_32.33 | all-reduce | flops 4 | bytes 32 | tf_op jit(solution)/shard_map/psum | solution.py:93
  637.5 19.3 %fusion.3 = f32[2,8,128,1152]{3,2,1,0:T(8,128)} fusion(bf16[8,2,128,2048]{3,2,1,0:T(8,128)(2,1)} %bitcast.252, bf16[2,2048,1152]{2,1,0:T(8,128)(2,1)} %param.7, pred[2048,1152]{1,0:T(8,128)(4,1)S(1)} %broadcast_and_fusion), kind=kOutput, calls=%fused_computation.8 | convolution fusion | flops 9668395008 | bytes 29622272 | tf_op jit(solution)/shard_map/tbf,rtcb->rtfc/dot_general | solution.py:67
  667.5 18.4 %fusion.9 = f32[2,8,128,1152]{3,2,1,0:T(8,128)} fusion(bf16[8,2,128,2048]{3,2,1,0:T(8,128)(2,1)} %bitcast.254, bf16[2,2048,1152]{2,1,0:T(8,128)(2,1)} %param.7, pred[2048,1152]{1,0:T(8,128)(4,1)S(1)} %broadcast_and_fusion), kind=kOutput, calls=%fused_computation.14 | convolution fusion | flops 9668395008 | bytes 29622272 | tf_op jit(solution)/shard_map/tbf,rtcb->rtfc/dot_general | solution.py:67
  696.1 27.7 %all-gather.11.cloned.1.call-done = bf16[16,128,2048]{2,1,0:T(8,128)(2,1)} async-done(((bf16[2,128,2048]{2,1,0:T(8,128)(2,1)}), bf16[16,128,2048]{2,1,0:T(8,128)(2,1)}) %all-gather.11.cloned.1.call-update) | async-done | bytes 8388624 | tf_op jit(solution)/shard_map/all_gather | solution.py:65
  747.6 18.5 %fusion.20 = f32[2,2048,1152,1]{2,1,0,3:T(8,128)} fusion(bf16[8,2,128,2048]{3,2,1,0:T(8,128)(2,1)} %bitcast.255, bf16[2,1152,8,128]{1,3,2,0:T(8,128)(2,1)} %get-tuple-element.36), kind=kOutput, calls=%fused_computation.33 | convolution fusion | flops 9663676416 | bytes 31981568 | tf_op jit(solution)/shard_map/rtcb,tfrc->tbf/dot_general | solution.py:74
  783.4 18.6 %fusion.16 = f32[2,2048,1152,1]{2,1,0,3:T(8,128)} fusion(bf16[8,2,128,2048]{3,2,1,0:T(8,128)(2,1)} %bitcast.256, bf16[2,1152,8,128]{1,3,2,0:T(8,128)(2,1)} %get-tuple-element.38), kind=kOutput, calls=%fused_computation.29 | convolution fusion | flops 9663676416 | bytes 31981568 | tf_op jit(solution)/shard_map/rtcb,tfrc->tbf/dot_general | solution.py:74
  802.0 28.0 %fusion.2 = bf16[2,2048,1152]{2,1,0:T(8,128)(2,1)} fusion(f32[2,2048,1152,1]{2,1,0,3:T(8,128)} %fusion.16, f32[2,2048,1152,1]{2,1,0,3:T(8,128)} %fusion.18, f32[2,2048,1152,1]{2,1,0,3:T(8,128)} %fusion.20, bf16[8,2,128,2048]{3,2,1,0:T(8,128)(2,1)} %bitcast.253, pred[2048,1152]{1,0:T(8,128)(4,1)S(1)} %broadcast_and_fusion, ...), kind=kOutput, calls=%fused_computation.4 | convolution fusion | flops 9687269376 | bytes 81526784 | tf_op jit(solution)/shard_map/rtcb,tfrc->tbf/dot_general | solution.py:74
  830.0 18.6 %fusion.5 = f32[2,8,128,1152]{3,2,1,0:T(8,128)} fusion(bf16[8,2,128,2048]{3,2,1,0:T(8,128)(2,1)} %bitcast.257, bf16[2,2048,1152]{2,1,0:T(8,128)(2,1)} %param.7, pred[2048,1152]{1,0:T(8,128)(4,1)S(1)} %broadcast_and_fusion), kind=kOutput, calls=%fused_computation.10 | convolution fusion | flops 9668395008 | bytes 29622272 | tf_op jit(solution)/shard_map/tbf,rtcb->rtfc/dot_general | solution.py:67
  864.9 19.2 %collective-permute-done.12 = bf16[2,2,1152,128]{2,3,0,1:T(8,128)(2,1)S(1)} collective-permute-done((bf16[2,2,1152,128]{2,3,0,1:T(8,128)(2,1)S(1)}, bf16[2,2,1152,128]{2,3,0,1:T(8,128)(2,1)S(1)}, u32[]{:S(2)}, u32[]{:S(2)}) %collective-permute-start.12) | collective-permute-done | bytes 1179680 | tf_op jit(solution)/shard_map/ppermute | solution.py:24
  887.2 22.2 %collective-permute-done.19 = bf16[2,2,1152,128]{2,3,0,1:T(8,128)(2,1)S(1)} collective-permute-done((bf16[2,2,1152,128]{2,3,0,1:T(8,128)(2,1)S(1)}, bf16[2,2,1152,128]{2,3,0,1:T(8,128)(2,1)S(1)}, u32[]{:S(2)}, u32[]{:S(2)}) %collective-permute-start.19) | collective-permute-done | bytes 1179680 | tf_op jit(solution)/shard_map/ppermute | solution.py:24
  966.6 18.8 %collective-permute-done.13 = bf16[2,2,1152,128]{2,3,0,1:T(8,128)(2,1)} collective-permute-done((bf16[2,2,1152,128]{2,3,0,1:T(8,128)(2,1)S(1)}, bf16[2,2,1152,128]{2,3,0,1:T(8,128)(2,1)}, u32[]{:S(2)}, u32[]{:S(2)}) %collective-permute-start.13) | collective-permute-done | bytes 1179680 | tf_op jit(solution)/shard_map/ppermute | solution.py:24
  993.3 28.3 %collective-permute-done.10 = bf16[2,2,1152,128]{2,3,0,1:T(8,128)(2,1)S(1)} collective-permute-done((bf16[2,2,1152,128]{2,3,0,1:T(8,128)(2,1)}, bf16[2,2,1152,128]{2,3,0,1:T(8,128)(2,1)S(1)}, u32[]{:S(2)}, u32[]{:S(2)}) %collective-permute-start.10) | collective-permute-done | bytes 1179680 | tf_op jit(solution)/shard_map/ppermute | solution.py:24
  1028.0 18.9 %collective-permute-done.16 = bf16[2,2,1152,128]{2,3,0,1:T(8,128)(2,1)S(1)} collective-permute-done((bf16[2,2,1152,128]{2,3,0,1:T(8,128)(2,1)}, bf16[2,2,1152,128]{2,3,0,1:T(8,128)(2,1)S(1)}, u32[]{:S(2)}, u32[]{:S(2)}) %collective-permute-start.16) | collective-permute-done | bytes 1179680 | tf_op jit(solution)/shard_map/ppermute | solution.py:24
  1053.1 19.1 %collective-permute-done.23 = bf16[2,2,1152,128]{2,3,0,1:T(8,128)(2,1)S(1)} collective-permute-done((bf16[2,2,1152,128]{2,3,0,1:T(8,128)(2,1)S(1)}, bf16[2,2,1152,128]{2,3,0,1:T(8,128)(2,1)S(1)}, u32[]{:S(2)}, u32[]{:S(2)}) %collective-permute-start.23) | collective-permute-done | bytes 1179680 | tf_op jit(solution)/shard_map/ppermute | solution.py:24
  1078.4 19.1 %collective-permute-done.5 = bf16[2,2,1152,128]{2,3,0,1:T(8,128)(2,1)S(1)} collective-permute-done((bf16[2,2,1152,128]{2,3,0,1:T(8,128)(2,1)S(1)}, bf16[2,2,1152,128]{2,3,0,1:T(8,128)(2,1)S(1)}, u32[]{:S(2)}, u32[]{:S(2)}) %collective-permute-start.5) | collective-permute-done | bytes 1179680 | tf_op jit(solution)/shard_map/ppermute | solution.py:24
  1099.5 23.2 %collective-permute-done.11 = bf16[2,2,1152,128]{2,3,0,1:T(8,128)(2,1)S(1)} collective-permute-done((bf16[2,2,1152,128]{2,3,0,1:T(8,128)(2,1)S(1)}, bf16[2,2,1152,128]{2,3,0,1:T(8,128)(2,1)S(1)}, u32[]{:S(2)}, u32[]{:S(2)}) %collective-permute-start.11) | collective-permute-done | bytes 1179680 | tf_op jit(solution)/shard_map/ppermute | solution.py:24
  1123.1 23.2 %collective-permute-done.17 = bf16[2,2,1152,128]{2,3,0,1:T(8,128)(2,1)S(1)} collective-permute-done((bf16[2,2,1152,128]{2,3,0,1:T(8,128)(2,1)S(1)}, bf16[2,2,1152,128]{2,3,0,1:T(8,128)(2,1)S(1)}, u32[]{:S(2)}, u32[]{:S(2)}) %collective-permute-start.17) | collective-permute-done | bytes 1179680 | tf_op jit(solution)/shard_map/ppermute | solution.py:24
  (167 shorter events, 312.0 us)
Async XLA Ops:
  7.2 176.7 %reduce-scatter.9.cloned.1.call-start = ((), (), s32[]{:S(2)}) async-start(), calls=%async_computation.6 | async-start | bytes 18874368 | tf_op jit(solution)/shard_map/reduce_scatter | solution.py:49
  66.6 236.8 %reduce-scatter.11.cloned.1.call-start = ((), (), s32[]{:S(2)}) async-start(), calls=%async_computation.7 | async-start | bytes 18874368 | tf_op jit(solution)/shard_map/reduce_scatter | solution.py:49
  86.4 336.7 %reduce-scatter.7.cloned.1.call-start = ((), (), s32[]{:S(2)}) async-start(), calls=%async_computation.5 | async-start | bytes 18874368 | tf_op jit(solution)/shard_map/reduce_scatter | solution.py:49
  107.1 435.4 %reduce-scatter.5.cloned.1.call-start = ((), (), s32[]{:S(2)}) async-start(), calls=%async_computation.4 | async-start | bytes 18874368 | tf_op jit(solution)/shard_map/reduce_scatter | solution.py:49
  125.5 511.9 %all-gather.15.cloned.1.call-start = ((), (), s32[]{:S(2)}) async-start(), calls=%async_computation.11 | async-start | bytes 9437184 | tf_op jit(solution)/shard_map/all_gather | solution.py:65
  556.4 111.1 %all-gather.9.cloned.1.call-start = ((), (), s32[]{:S(2)}) async-start(), calls=%async_computation.8 | async-start | bytes 9437184 | tf_op jit(solution)/shard_map/all_gather | solution.py:65
  557.0 166.8 %all-gather.11.cloned.1.call-start = ((), (), s32[]{:S(2)}) async-start(), calls=%async_computation.9 | async-start | bytes 9437184 | tf_op jit(solution)/shard_map/all_gather | solution.py:65
  557.7 225.6 %all-gather.13.cloned.1.call-start = ((), (), s32[]{:S(2)}) async-start(), calls=%async_computation.10 | async-start | bytes 9437184 | tf_op jit(solution)/shard_map/all_gather | solution.py:65
  660.9 190.5 %collective-permute-start.18 = (bf16[2,2,1152,128]{2,3,0,1:T(8,128)(2,1)}, bf16[2,2,1152,128]{2,3,0,1:T(8,128)(2,1)}, u32[]{:S(2)}, u32[]{:S(2)}) collective-permute-start(bf16[2,2,1152,128]{2,3,0,1:T(8,128)(2,1)} %get-tuple-element.54), channel_id=1, source_target_pairs={{0,8},{1,9},{2,10},{3,11},{4,12},{5,13},{6,14},{7,15}} | collective-permute-start | bytes 3538952 | tf_op jit(solution)/shard_map/ppermute | solution.py:24
  662.2 224.1 %collective-permute-start.21 = (bf16[2,2,1152,128]{2,3,0,1:T(8,128)(2,1)}, bf16[2,2,1152,128]{2,3,0,1:T(8,128)(2,1)}, u32[]{:S(2)}, u32[]{:S(2)}) collective-permute-start(bf16[2,2,1152,128]{2,3,0,1:T(8,128)(2,1)} %get-tuple-element.55), channel_id=1, source_target_pairs={{24,16},{25,17},{26,18},{27,19},{28,20},{29,21},{30,22},{31,23}} | collective-permute-start | bytes 3538952 | tf_op jit(solution)/shard_map/ppermute | solution.py:24
  693.1 168.0 %collective-permute-start = (bf16[2,2,1152,128]{2,3,0,1:T(8,128)(2,1)}, bf16[2,2,1152,128]{2,3,0,1:T(8,128)(2,1)}, u32[]{:S(2)}, u32[]{:S(2)}) collective-permute-start(bf16[2,2,1152,128]{2,3,0,1:T(8,128)(2,1)} %get-tuple-element.42), channel_id=1, source_target_pairs={{0,8},{1,9},{2,10},{3,11},{4,12},{5,13},{6,14},{7,15}} | collective-permute-start | bytes 3538952 | tf_op jit(solution)/shard_map/ppermute | solution.py:24
  694.4 222.6 %collective-permute-start.3 = (bf16[2,2,1152,128]{2,3,0,1:T(8,128)(2,1)}, bf16[2,2,1152,128]{2,3,0,1:T(8,128)(2,1)}, u32[]{:S(2)}, u32[]{:S(2)}) collective-permute-start(bf16[2,2,1152,128]{2,3,0,1:T(8,128)(2,1)} %get-tuple-element.43), channel_id=1, source_target_pairs={{24,16},{25,17},{26,18},{27,19},{28,20},{29,21},{30,22},{31,23}} | collective-permute-start | bytes 3538952 | tf_op jit(solution)/shard_map/ppermute | solution.py:24
  745.9 109.6 %collective-permute-start.6 = (bf16[2,2,1152,128]{2,3,0,1:T(8,128)(2,1)}, bf16[2,2,1152,128]{2,3,0,1:T(8,128)(2,1)}, u32[]{:S(2)}, u32[]{:S(2)}) collective-permute-start(bf16[2,2,1152,128]{2,3,0,1:T(8,128)(2,1)} %get-tuple-element.46), channel_id=1, source_target_pairs={{0,8},{1,9},{2,10},{3,11},{4,12},{5,13},{6,14},{7,15}} | collective-permute-start | bytes 3538952 | tf_op jit(solution)/shard_map/ppermute | solution.py:24
  855.5 54.0 %collective-permute-start.19 = (bf16[2,2,1152,128]{2,3,0,1:T(8,128)(2,1)S(1)}, bf16[2,2,1152,128]{2,3,0,1:T(8,128)(2,1)S(1)}, u32[]{:S(2)}, u32[]{:S(2)}) collective-permute-start(bf16[2,2,1152,128]{2,3,0,1:T(8,128)(2,1)S(1)} %fusion.24), channel_id=1, source_target_pairs={{0,8},{8,16},{1,9},{9,17},{2,10},{10,18},{3,11},{11,19},{4,12},{12... | collective-permute-start | bytes 3538952 | tf_op jit(solution)/shard_map/ppermute | solution.py:24
  861.2 80.2 %collective-permute-start.9 = (bf16[2,2,1152,128]{2,3,0,1:T(8,128)(2,1)S(1)}, bf16[2,2,1152,128]{2,3,0,1:T(8,128)(2,1)}, u32[]{:S(2)}, u32[]{:S(2)}) collective-permute-start(bf16[2,2,1152,128]{2,3,0,1:T(8,128)(2,1)S(1)} %get-tuple-element.47), channel_id=1, source_target_pairs={{24,16},{25,17},{26,18},{27,19},{28,20},{29,21},{30,22},{31,23}} | collective-permute-start | bytes 3538952 | tf_op jit(solution)/shard_map/ppermute | solution.py:24
  886.3 79.0 %collective-permute-start.15 = (bf16[2,2,1152,128]{2,3,0,1:T(8,128)(2,1)S(1)}, bf16[2,2,1152,128]{2,3,0,1:T(8,128)(2,1)S(1)}, u32[]{:S(2)}, u32[]{:S(2)}) collective-permute-start(bf16[2,2,1152,128]{2,3,0,1:T(8,128)(2,1)S(1)} %get-tuple-element.51), channel_id=1, source_target_pairs={{24,16},{25,17},{26,18},{27,19},{28,20},{29,21},{30,22},{31,23}} | collective-permute-start | bytes 3538952 | tf_op jit(solution)/shard_map/ppermute | solution.py:24
  917.0 68.4 %collective-permute-start.13 = (bf16[2,2,1152,128]{2,3,0,1:T(8,128)(2,1)S(1)}, bf16[2,2,1152,128]{2,3,0,1:T(8,128)(2,1)}, u32[]{:S(2)}, u32[]{:S(2)}) collective-permute-start(bf16[2,2,1152,128]{2,3,0,1:T(8,128)(2,1)S(1)} %fusion.28), channel_id=1, source_target_pairs={{0,8},{8,16},{1,9},{9,17},{2,10},{10,18},{3,11},{11,19},{4,12},{12... | collective-permute-start | bytes 3538952 | tf_op jit(solution)/shard_map/ppermute | solution.py:24
  935.7 113.4 %collective-permute-start.20 = (bf16[2,2,1152,128]{2,3,0,1:T(8,128)(2,1)S(1)}, bf16[2,2,1152,128]{2,3,0,1:T(8,128)(2,1)S(1)}, u32[]{:S(2)}, u32[]{:S(2)}) collective-permute-start(bf16[2,2,1152,128]{2,3,0,1:T(8,128)(2,1)S(1)} %get-tuple-element.52), channel_id=1, source_target_pairs={{0,8},{8,16},{16,24},{1,9},{9,17},{17,25},{2,10},{10,18},{18,26},{... | collective-permute-start | bytes 3538952 | tf_op jit(solution)/shard_map/ppermute | solution.py:24
  960.1 116.4 %collective-permute-start.2 = (bf16[2,2,1152,128]{2,3,0,1:T(8,128)(2,1)}, bf16[2,2,1152,128]{2,3,0,1:T(8,128)(2,1)S(1)}, u32[]{:S(2)}, u32[]{:S(2)}) collective-permute-start(bf16[2,2,1152,128]{2,3,0,1:T(8,128)(2,1)} %get-tuple-element.40), channel_id=1, source_target_pairs={{0,8},{8,16},{16,24},{1,9},{9,17},{17,25},{2,10},{10,18},{18,26},{... | collective-permute-start | bytes 3538952 | tf_op jit(solution)/shard_map/ppermute | solution.py:24
  965.3 58.4 %collective-permute-start.4 = (bf16[2,2,1152,128]{2,3,0,1:T(8,128)(2,1)}, bf16[2,2,1152,128]{2,3,0,1:T(8,128)(2,1)S(1)}, u32[]{:S(2)}, u32[]{:S(2)}) collective-permute-start(bf16[2,2,1152,128]{2,3,0,1:T(8,128)(2,1)} %get-tuple-element.41), channel_id=1, source_target_pairs={{24,16},{16,8},{25,17},{17,9},{26,18},{18,10},{27,19},{19,11},{28,... | collective-permute-start | bytes 3538952 | tf_op jit(solution)/shard_map/ppermute | solution.py:24
  990.0 56.9 %collective-permute-start.16 = (bf16[2,2,1152,128]{2,3,0,1:T(8,128)(2,1)}, bf16[2,2,1152,128]{2,3,0,1:T(8,128)(2,1)S(1)}, u32[]{:S(2)}, u32[]{:S(2)}) collective-permute-start(bf16[2,2,1152,128]{2,3,0,1:T(8,128)(2,1)} %get-tuple-element.49), channel_id=1, source_target_pairs={{24,16},{16,8},{25,17},{17,9},{26,18},{18,10},{27,19},{19,11},{28,... | collective-permute-start | bytes 3538952 | tf_op jit(solution)/shard_map/ppermute | solution.py:24
  1023.8 75.7 %collective-permute-start.8 = (bf16[2,2,1152,128]{2,3,0,1:T(8,128)(2,1)S(1)}, bf16[2,2,1152,128]{2,3,0,1:T(8,128)(2,1)S(1)}, u32[]{:S(2)}, u32[]{:S(2)}) collective-permute-start(bf16[2,2,1152,128]{2,3,0,1:T(8,128)(2,1)S(1)} %get-tuple-element.44), channel_id=1, source_target_pairs={{0,8},{8,16},{16,24},{1,9},{9,17},{17,25},{2,10},{10,18},{18,26},{... | collective-permute-start | bytes 3538952 | tf_op jit(solution)/shard_map/ppermute | solution.py:24
  1049.1 74.0 %collective-permute-start.14 = (bf16[2,2,1152,128]{2,3,0,1:T(8,128)(2,1)S(1)}, bf16[2,2,1152,128]{2,3,0,1:T(8,128)(2,1)S(1)}, u32[]{:S(2)}, u32[]{:S(2)}) collective-permute-start(bf16[2,2,1152,128]{2,3,0,1:T(8,128)(2,1)S(1)} %copy-done.14), channel_id=1, source_target_pairs={{0,8},{8,16},{16,24},{1,9},{9,17},{17,25},{2,10},{10,18},{18,26},{... | collective-permute-start | bytes 3538952 | tf_op jit(solution)/shard_map/ppermute | solution.py:24
  1076.5 69.9 %collective-permute-start.17 = (bf16[2,2,1152,128]{2,3,0,1:T(8,128)(2,1)S(1)}, bf16[2,2,1152,128]{2,3,0,1:T(8,128)(2,1)S(1)}, u32[]{:S(2)}, u32[]{:S(2)}) collective-permute-start(bf16[2,2,1152,128]{2,3,0,1:T(8,128)(2,1)S(1)} %fusion.27), channel_id=1, source_target_pairs={{24,16},{16,8},{8,0},{25,17},{17,9},{9,1},{26,18},{18,10},{10,2},{... | collective-permute-start | bytes 3538952 | tf_op jit(solution)/shard_map/ppermute | solution.py:24
  (35 other events, 1021.2 us)
Sparse Core Ops, SparseCore 0:
  66.8 117.1 reduce-scatter.8
  187.5 115.9 reduce-scatter.10
  307.0 115.9 reduce-scatter.6
  426.4 115.9 reduce-scatter.4
  556.5 54.7 all-gather.14
  613.0 54.4 all-gather.8
  669.4 54.3 all-gather.10
  725.7 54.3 all-gather.12

commit v2 on v1

--- a/solution.py
+++ b/solution.py
@@ -1,14 +1,594 @@
+import functools
+
 import jax
 import jax.numpy as jnp
 from jax import lax
+from jax.experimental import pallas as pl
+from jax.experimental.pallas import tpu as pltpu
 from jax.sharding import PartitionSpec as P
 
 F = 9216
 C = 4096
 BLOCK = 128
-
-
-def chain(own, up):
+STEP = 64
+IMAGES = 256
+SLOTS = 4
+F32 = jnp.float32
+BF16 = jnp.bfloat16
+MESH = pl.DeviceIdType.MESH
+
+
+def fold(value):
+    return sum(value[:, i : i + 128] for i in range(0, value.shape[1], 128))
+
+
+def kernel(
+    planes,
+    x_hbm,
+    wt_hbm,
+    cot_hbm,
+    small_ref,
+    pad_ref,
+    valid_ref,
+    bias_ref,
+    stitch_ref,
+    st_hbm,
+    g_hbm,
+    gw_hbm,
+    gb_ref,
+    gs_ref,
+    sq_ref,
+    xb,
+    wo,
+    wp,
+    part,
+    r1,
+    r2,
+    gfull,
+    cbuf,
+    stbuf,
+    zo,
+    zsend,
+    zrecv,
+    zfin,
+    x_sem,
+    xs_sem,
+    xr_sem,
+    wo_sem,
+    ws_sem,
+    wr_sem,
+    rs1_s,
+    rs1_r,
+    rs2_s,
+    rs2_r,
+    ag1_s,
+    ag1_r,
+    ag2_s,
+    ag2_r,
+    cx_s,
+    cx_r,
+    c_sem,
+    st_sem,
+    g_sem,
+    z_s,
+    z_r,
+    zf_sem,
+):
+    towers, images, width = x_hbm.shape
+    chunks = cot_hbm.shape[1]
+    per_chunk = images // IMAGES
+    total = chunks * per_chunk
+    last = planes - 1
+
+    z = lax.axis_index("dp")
+    row = lax.axis_index("rows")
+    y = row // 4
+    x = (row // 2) % 2
+    core = row % 2
+    oy, ox, oc = 1 - y, 1 - x, 1 - core
+    to_x = (z, y * 4 + ox * 2 + core)
+    to_y = (z, oy * 4 + x * 2 + core)
+    to_core = (z, y * 4 + x * 2 + oc)
+
+    barrier = pltpu.get_barrier_semaphore()
+    for there in (to_x, to_y, to_core):
+        pl.semaphore_signal(barrier, inc=1, device_id=there, device_id_type=MESH)
+
+    @pl.when(z > 0)
+    def _():
+        pl.semaphore_signal(barrier, inc=1, device_id=(z - 1, row), device_id_type=MESH)
+
+    @pl.when(z < last)
+    def _():
+        pl.semaphore_signal(barrier, inc=1, device_id=(z + 1, row), device_id_type=MESH)
+
+    def remote(src, dst, send, recv, there):
+        return pltpu.make_async_remote_copy(
+            src_ref=src, dst_ref=dst, send_sem=send, recv_sem=recv, device_id=there, device_id_type=MESH
+        )
+
+    def lanes(q):
+        return pl.ds(pl.multiple_of((q % per_chunk) * IMAGES, IMAGES), IMAGES)
+
+    def x_local(i):
+        cut = pl.ds(i * IMAGES, IMAGES)
+        return pltpu.make_async_copy(x_hbm.at[:, cut], xb.at[0, :, cut], x_sem.at[i])
+
+    def x_remote(i):
+        cut = pl.ds(i * IMAGES, IMAGES)
+        return remote(x_hbm.at[:, cut], xb.at[1, :, cut], xs_sem.at[i], xr_sem.at[i], to_core)
+
+    def w_local(k):
+        return pltpu.make_async_copy(wt_hbm.at[:, :, core, k], wo.at[k % 2], wo_sem.at[k % 2])
+
+    def w_remote(k):
+        return remote(wt_hbm.at[:, :, oc, k], wp.at[k], ws_sem.at[k], wr_sem.at[k], to_core)
+
+    def rs1(q):
+        s = q % SLOTS
+        return (
+            remote(part.at[s, :, ox, 0], r1.at[s, 0], rs1_s.at[s, 0], rs1_r.at[s, 0], to_x),
+            remote(part.at[s, oy, :, 1], r1.at[s, 1], rs1_s.at[s, 1], rs1_r.at[s, 1], to_y),
+        )
+
+    def rs2(q):
+        s = q % SLOTS
+        return (
+            remote(part.at[s, oy, x, 0], r2.at[s, 0], rs2_s.at[s, 0], rs2_r.at[s, 0], to_y),
+            remote(part.at[s, y, ox, 1], r2.at[s, 1], rs2_s.at[s, 1], rs2_r.at[s, 1], to_x),
+        )
+
+    def ag1(q):
+        s, c, cut = q % SLOTS, (q // per_chunk) % 2, lanes(q)
+        a = gfull.at[c, 0, y, x, core, :, cut]
+        b = gfull.at[c, 1, y, x, core, :, cut]
+        return (
+            remote(a, a, ag1_s.at[s, 0], ag1_r.at[s, 0], to_x),
+            remote(b, b, ag1_s.at[s, 1], ag1_r.at[s, 1], to_y),
+        )
+
+    def ag2(q):
+        s, c, cut = q % SLOTS, (q // per_chunk) % 2, lanes(q)
+        a = gfull.at[c, 0, y, :, core, :, cut]
+        b = gfull.at[c, 1, :, x, core, :, cut]
+        return (
+            remote(a, a, ag2_s.at[s, 0], ag2_r.at[s, 0], to_y),
+            remote(b, b, ag2_s.at[s, 1], ag2_r.at[s, 1], to_x),
+        )
+
+    def cx(q):
+        s, c, cut = q % SLOTS, (q // per_chunk) % 2, lanes(q)
+        a = gfull.at[c, :, :, :, core, :, cut]
+        return (remote(a, a, cx_s.at[s], cx_r.at[s], to_core),)
+
+    def cot_copy(q):
+        s = q % SLOTS
+        return pltpu.make_async_copy(cot_hbm.at[:, q // per_chunk, :, lanes(q)], cbuf.at[s], c_sem.at[s])
+
+    def st_copy(q):
+        s = q % SLOTS
+        return pltpu.make_async_copy(stbuf.at[s], st_hbm.at[:, q // per_chunk, :, lanes(q)], st_sem.at[s])
+
+    def g_copy(k):
+        return pltpu.make_async_copy(gfull.at[k % 2], g_hbm.at[:, :, :, :, k], g_sem.at[k % 2])
+
+    def gw_copy(k):
+        return pltpu.make_async_copy(zfin, gw_hbm.at[:, :, k], zf_sem)
+
+    def z_slot(k, j):
+        return j if j < planes - 2 else j + k % 2
+
+    def z_copy(k, j, way):
+        n = z_slot(k, j)
+        there = (z + 1, row) if way == 0 else (z - 1, row)
+        return remote(zsend.at[way, j], zrecv.at[way, n], z_s.at[way, j], z_r.at[way, n], there)
+
+    def start(copies):
+        for c in copies:
+            c.start()
+
+    def wait_send(copies):
+        for c in copies:
+            c.wait_send()
+
+    def wait_recv(copies):
+        for c in copies:
+            c.wait_recv()
+
+    def stage(q, work, sends, *sent):
+        @pl.when((q >= SLOTS) & (q < total + SLOTS))
+        def _():
+            for copies in sent:
+                wait_send(copies(q - SLOTS))
+
+        @pl.when((q >= 0) & (q < total))
+        def _():
+            work(q)
+            start(sends(q))
+
+    def forward(q):
+        k, i, s = q // per_chunk, q % per_chunk, q % SLOTS
+
+        cot_copy(q).start()
+
+        @pl.when(i == 0)
+        def _():
+            w_local(k).wait()
+            w_remote(k).wait_recv()
+
+            @pl.when(k + 1 < chunks)
+            def _():
+                w_local(k + 1).start()
+
+        cut = pl.ds(pl.multiple_of(i * IMAGES, IMAGES), IMAGES)
+
+        @pl.when(k == 0)
+        def _():
+            x_local(i).wait()
+            x_remote(i).wait_recv()
+            keep = (1.0 - small_ref[cut, :] * pad_ref[...]).astype(BF16)
+            for side in range(2):
+                for t in range(towers):
+                    xb[side, t, cut] = xb[side, t, cut] * keep
+
+        for t in range(towers):
+            out = lax.dot_general(
+                wo[k % 2, t].reshape(4 * STEP, width),
+                xb[0, t, cut],
+                (((1,), (1,)), ((), ())),
+                preferred_element_type=F32,
+            ) + lax.dot_general(
+                wp[k, t].reshape(4 * STEP, width),
+                xb[1, t, cut],
+                (((1,), (1,)), ((), ())),
+                preferred_element_type=F32,
+            )
+            out = out.reshape(2, 2, STEP, IMAGES)
+            for a in range(2):
+                for b in range(2):
+                    part[s, a, b, t] = out[a, b]
+
+    def reduce(q):
+        s = q % SLOTS
+        wait_recv(rs1(q))
+        part[s, oy, x, 0] = part[s, oy, x, 0] + r1[s, 0, oy]
+        part[s, y, ox, 1] = part[s, y, ox, 1] + r1[s, 1, ox]
+        part[s, y, x, 0] = part[s, y, x, 0] + r1[s, 0, y]
+        part[s, y, x, 1] = part[s, y, x, 1] + r1[s, 1, x]
+
+    def pointwise(q):
+        k, i, s = q // per_chunk, q % per_chunk, q % SLOTS
+        wait_recv(rs2(q))
+        cot_copy(q).wait()
+
+        @pl.when(q >= SLOTS)
+        def _():
+            st_copy(q - SLOTS).wait()
+
+        valid = valid_ref[i]
+        pre = [part[s, y, x, t] + r2[s, t] + bias_ref[t, k] for t in range(2)]
+        act = [jnp.maximum(p, 0.0) for p in pre]
+        up = [cbuf[s, t].astype(F32) * valid for t in range(2)]
+        cut = lanes(q)
+        for a in range(2):
+            out = stitch_ref[a, 0, k] * act[0] + stitch_ref[a, 1, k] * act[1]
+            stbuf[s, a] = out.astype(BF16)
+            sq_ref[1] = sq_ref[1] + fold(out * out * valid)
+            for b in range(2):
+                gs_ref[k, a, b] = gs_ref[k, a, b] + fold(up[a] * act[b])
+        for t in range(2):
+            sq_ref[0] = sq_ref[0] + fold(pre[t] * pre[t] * valid)
+            grad = stitch_ref[0, t, k] * up[0] + stitch_ref[1, t, k] * up[1]
+            grad = jnp.where(pre[t] > 0, grad, 0.0).astype(BF16)
+            gfull[k % 2, t, y, x, core, :, cut] = grad
+            gb_ref[k, t] = gb_ref[k, t] + fold(grad.astype(F32))
+        st_copy(q).start()
+
+    def spread(q):
+        wait_recv(ag1(q))
+
+    def across(q):
+        wait_recv(ag2(q))
+
+    def terms(k, n):
+        third = width // 3
+        for t in range(towers):
+            value = jnp.dot(
+                gfull[k % 2, t].reshape(8 * STEP, images),
+                xb[0, t, :, n * third : (n + 1) * third],
+                preferred_element_type=F32,
+            )
+            value = value.astype(BF16).reshape(planes, 8 // planes, STEP, third)
+            for d in range(planes):
+                for e in range(8 // planes):
+                    zo[t, d, e, :, n * third : (n + 1) * third] = value[d, e]
+
+    halves = 8 // planes
+
+    def chain(k, j):
+        for way in range(2):
+            near = z if way == 0 else last - z
+            got = z_copy(k, j - 1, way) if j > 0 else None
+            if j > 0:
+
+                @pl.when((near >= 1) & (near <= j))
+                def _():
+                    got.wait_recv()
+
+            if j <= planes - 2:
+
+                @pl.when(near <= j)
+                def _():
+                    dest = last - j + z if way == 0 else j - last + z
+
+                    @pl.when(k > 0)
+                    def _():
+                        z_copy(k - 1, j, way).wait_send()
+
+                    if j > 0:
+                        n = z_slot(k, j - 1)
+
+                        @pl.when(near >= 1)
+                        def _():
+                            def add(i, carry):
+                                t, e = i // halves, i % halves
+                                value = zo[t, dest, e].astype(F32) + zrecv[way, n, t, e].astype(F32)
+                                zsend[way, j, t, e] = value.astype(BF16)
+                                return carry
+
+                            lax.fori_loop(0, towers * halves, add, 0)
+
+                        @pl.when(near == 0)
+                        def _():
+                            zsend[way, j] = zo[:, dest]
+
+                    else:
+                        zsend[way, j] = zo[:, dest]
+
+        for way in range(2):
+            near = z if way == 0 else last - z
+            if j <= planes - 2:
+
+                @pl.when(near <= j)
+                def _():
+                    z_copy(k, j, way).start()
+
+        if j == planes - 2:
+
+            @pl.when(k > 0)
+            def _():
+                gw_copy(k - 1).wait()
+
+            def begin(i, carry):
+                t, e = i // halves, i % halves
+                zfin[t, e] = zo[t, z, e].astype(F32)
+                return carry
+
+            lax.fori_loop(0, towers * halves, begin, 0)
+        if j == planes - 1:
+            n = z_slot(k, j - 1)
+            for way in range(2):
+                near = z if way == 0 else last - z
+
+                @pl.when(near >= 1)
+                def _():
+                    def more(i, carry):
+                        t, e = i // halves, i % halves
+                        zfin[t, e] = zfin[t, e] + zrecv[way, n, t, e].astype(F32)
+                        return carry
+
+                    lax.fori_loop(0, towers * halves, more, 0)
+
+            gw_copy(k).start()
+
+    x_local(0).start()
+    w_local(0).start()
+    for i in range(1, per_chunk):
+        x_local(i).start()
+    pl.semaphore_wait(barrier, 3 + jnp.minimum(z, 1) + jnp.minimum(last - z, 1))
+    w_remote(0).start()
+
+    def send_x(i, carry):
+        x_remote(i).start()
+        return carry
+
+    lax.fori_loop(0, per_chunk, send_x, 0)
+
+    def send_w(k, carry):
+        w_remote(k).start()
+        return carry
+
+    lax.fori_loop(1, chunks, send_w, 0)
+    gb_ref[...] = jnp.zeros_like(gb_ref)
+    gs_ref[...] = jnp.zeros_like(gs_ref)
+    sq_ref[...] = jnp.zeros_like(sq_ref)
+
+    ready = per_chunk - 1 + 5
+    space = per_chunk // 4
+    offsets = [2 + j * space for j in range(planes)]
+
+    def body(s, carry):
+        stage(s, forward, rs1, rs1, rs2)
+        stage(s - 1, reduce, rs2)
+        stage(s - 2, pointwise, ag1, ag1)
+        stage(s - 3, spread, ag2, ag2)
+        stage(s - 4, across, cx, cx)
+
+        @pl.when((s >= 5) & (s < total + 5))
+        def _():
+            wait_recv(cx(s - 5))
+
+        @pl.when(s >= ready)
+        def _():
+            done = s - ready
+            k = done // per_chunk
+            at = done % per_chunk
+
+            for n in range(3):
+
+                @pl.when((at == n) & (k < chunks))
+                def _():
+                    if n == 0:
+                        g_copy(k).start()
+                    terms(k, n)
+                    if n == 2:
+                        g_copy(k).wait()
+
+            for j, off in enumerate(offsets):
+
+                @pl.when((done >= off) & ((done - off) % per_chunk == 0) & ((done - off) // per_chunk < chunks))
+                def _():
+                    chain((done - off) // per_chunk, j)
+
+        return carry
+
+    lax.fori_loop(0, total + ready - per_chunk + 1 + offsets[-1] + 1, body, 0)
+
+    def drain(q, carry):
+        st_copy(q).wait()
+        return carry
+
+    lax.fori_loop(total - SLOTS, total, drain, 0)
+
+    def drain_x(i, carry):
+        x_remote(i).wait_send()
+        return carry
+
+    lax.fori_loop(0, per_chunk, drain_x, 0)
+
+    def drain_w(k, carry):
+        w_remote(k).wait_send()
+        return carry
+
+    lax.fori_loop(0, chunks, drain_w, 0)
+    gw_copy(chunks - 1).wait()
+    for way in range(2):
+        near = z if way == 0 else last - z
+        for j in range(planes - 1):
+
+            @pl.when(near <= j)
+            def _():
+                z_copy(chunks - 1, j, way).wait_send()
+
+
+def fused(inputs, weights, bias, stitch, cotangent, valid, size_class):
+    planes = lax.axis_size("dp")
+    towers, images, width = inputs.shape
+    mine = bias.shape[1]
+    chunks = mine // STEP
+    per_chunk = images // IMAGES
+    halves = 8 // planes
+    small = (size_class == 195).astype(F32)[:, None]
+    place = lax.iota(jnp.int32, width) % 36
+    padded = ((place // 6 == 5) | (place % 6 == 5)).astype(F32)[None, :]
+    weight_valid = valid.astype(F32)
+    turned = jnp.transpose(weights, (0, 2, 1)).reshape(towers, 4, 2, chunks, STEP, width)
+    vmem = pl.BlockSpec(memory_space=pltpu.VMEM)
+    hbm = pl.BlockSpec(memory_space=pl.ANY)
+    dma = pltpu.SemaphoreType.DMA
+    zslots = planes
+    outs = pl.pallas_call(
+        functools.partial(kernel, planes),
+        out_shape=(
+            jax.ShapeDtypeStruct((2, chunks, STEP, images), BF16),
+            jax.ShapeDtypeStruct((2, 2, 2, 2, chunks, STEP, images), BF16),
+            jax.ShapeDtypeStruct((2, halves, chunks, STEP, width), F32),
+            jax.ShapeDtypeStruct((chunks, 2, STEP, 128), F32),
+            jax.ShapeDtypeStruct((chunks, 2, 2, STEP, 128), F32),
+            jax.ShapeDtypeStruct((2, STEP, 128), F32),
+        ),
+        in_specs=[hbm] * 3 + [vmem] * 5,
+        out_specs=(hbm, hbm, hbm, vmem, vmem, vmem),
+        scratch_shapes=[
+            pltpu.VMEM((2, towers, images, width), BF16),
+            pltpu.VMEM((2, towers, 4, STEP, width), BF16),
+            pltpu.VMEM((chunks, towers, 4, STEP, width), BF16),
+            pltpu.VMEM((SLOTS, 2, 2, towers, STEP, IMAGES), F32),
+            pltpu.VMEM((SLOTS, 2, 2, STEP, IMAGES), F32),
+            pltpu.VMEM((SLOTS, 2, STEP, IMAGES), F32),
+            pltpu.VMEM((2, towers, 2, 2, 2, STEP, images), BF16),
+            pltpu.VMEM((SLOTS, 2, STEP, IMAGES), BF16),
+            pltpu.VMEM((SLOTS, 2, STEP, IMAGES), BF16),
+            pltpu.VMEM((towers, planes, halves, STEP, width), BF16),
+            pltpu.VMEM((2, planes - 1, towers, halves, STEP, width), BF16),
+            pltpu.VMEM((2, zslots, towers, halves, STEP, width), BF16),
+            pltpu.VMEM((towers, halves, STEP, width), F32),
+            dma((per_chunk,)),
+            dma((per_chunk,)),
+            dma((per_chunk,)),
+            dma((2,)),
+            dma((chunks,)),
+            dma((chunks,)),
+            dma((SLOTS, 2)),
+            dma((SLOTS, 2)),
+            dma((SLOTS, 2)),
+            dma((SLOTS, 2)),
+            dma((SLOTS, 2)),
+            dma((SLOTS, 2)),
+            dma((SLOTS, 2)),
+            dma((SLOTS, 2)),
+            dma((SLOTS,)),
+            dma((SLOTS,)),
+            dma((SLOTS,)),
+            dma((SLOTS,)),
+            dma((2,)),
+            dma((2, planes - 1)),
+            dma((2, zslots)),
+            dma,
+        ],
+        compiler_params=pltpu.CompilerParams(
+            collective_id=0, has_side_effects=True, vmem_limit_bytes=67043328
+        ),
+        name="towers",
+    )(
+        inputs,
+        turned,
+        cotangent.reshape(2, chunks, STEP, images),
+        small,
+        padded,
+        weight_valid.reshape(per_chunk, 1, IMAGES),
+        bias.reshape(2, chunks, STEP, 1),
+        stitch.reshape(2, 2, chunks, STEP, 1),
+    )
+    stitched, gathered, grad_weights, grad_bias, grad_stitch, squares = outs
+    keep = 1.0 - small * padded
+    gathered = gathered.reshape(towers, -1, images)
+    total_x = jnp.einsum("tcb,tfc->tbf", gathered, weights, preferred_element_type=F32)
+    grad_inputs = (total_x * keep[None]).astype(BF16)
+    grad_weights = jnp.transpose(grad_weights.reshape(towers, -1, width), (0, 2, 1))
+    used_wide = inputs.astype(F32) * keep[None]
+    partial_value = jnp.stack(
+        [
+            jnp.sum(weight_valid[None, :, None] * used_wide * used_wide),
+            jnp.sum(squares[0]),
+            jnp.sum(squares[1]),
+            jnp.sum(weight_valid),
+        ]
+    )
+    grad_bias = jnp.transpose(jnp.sum(grad_bias, axis=3), (1, 0, 2)).reshape(2, mine)
+    grad_stitch = jnp.transpose(jnp.sum(grad_stitch, axis=4), (1, 2, 0, 3)).reshape(2, 2, mine)
+    grad_bias, grad_stitch = lax.psum((grad_bias, grad_stitch), "dp")
+    totals = lax.psum(partial_value, ("dp", "rows"))
+    return (
+        stitched.reshape(2, mine, images),
+        grad_inputs,
+        grad_weights,
+        grad_bias,
+        grad_stitch,
+        rms(totals),
+    )
+
+
+def rms(totals):
+    count = totals[3] / lax.axis_size("rows")
+    return jnp.sqrt(
+        jnp.stack(
+            [totals[0] / (count * 2 * F), totals[1] / (count * 2 * C), totals[2] / (count * 2 * C)]
+        )
+    )
+
+
+def line_sum(own, up):
     size = lax.axis_size("dp")
     here = lax.axis_index("dp")
     got = None
@@ -25,7 +605,7 @@
     return got
 
 
-def per_device(inputs, weights, bias, stitch, cotangent, valid, size_class):
+def plain(inputs, weights, bias, stitch, cotangent, valid, size_class):
     rows = lax.axis_size("rows")
     size = lax.axis_size("dp")
     here = lax.axis_index("dp")
@@ -68,7 +648,7 @@
         block = block.reshape(size, rows // size, 2, width, step)
         own = block.astype(jnp.bfloat16)
         total = lax.dynamic_index_in_dim(block, here, 0, keepdims=False)
-        total = total + chain(own, True).astype(jnp.float32) + chain(own, False).astype(jnp.float32)
+        total = total + line_sum(own, True).astype(jnp.float32) + line_sum(own, False).astype(jnp.float32)
         grad_weights.append(total)
     total_x = sum(
         jnp.einsum("rtcb,tfrc->tbf", pieces[k], mats[k], preferred_element_type=jnp.float32)
@@ -91,13 +671,11 @@
     )
     grad_bias, grad_stitch = lax.psum((grad_bias, grad_stitch), "dp")
     totals = lax.psum(partial_value, ("dp", "rows"))
-    count = totals[3] / rows
-    rms_values = jnp.sqrt(
-        jnp.stack(
-            [totals[0] / (count * 2 * F), totals[1] / (count * 2 * C), totals[2] / (count * 2 * C)]
-        )
-    )
-    return (stitched, grad_inputs, grad_weights, grad_bias, grad_stitch, rms_values)
+    return (stitched, grad_inputs, grad_weights, grad_bias, grad_stitch, rms(totals))
+
+
+def small_plane(mesh):
+    return mesh.shape["rows"] == 8 and mesh.shape["dp"] in (2, 4, 8)
 
 
 def solution(mesh):
@@ -119,5 +697,5 @@
         P(),
     )
     return jax.shard_map(
-        per_device, mesh=mesh, in_specs=in_specs, out_specs=out_specs, check_vma=False
-    )
+        fused if small_plane(mesh) else plain, mesh=mesh, in_specs=in_specs, out_specs=out_specs, check_vma=False
+    )

time: 1190 us -> 687 us (0.58)
  waiting for transfers between devices: 659 us -> 0 us
  Pallas kernels: 0 us -> 486 us
  matrix products: 233 us -> 67.6 us
  other arithmetic: 80.9 us -> 18.6 us
  starting transfers between devices: 47.3 us -> 0 us
  local copies, waits for them, and re-layouts: 83.2 us -> 48.1 us
  between operations: 23.6 us -> 3.97 us
    pallas_call x0 -> x1, Pallas kernels: none -> 486 us  [fused(): pl.pallas_call(functools.partial(kernel, planes), out_shape=(jax.ShapeDty...]
    reduce_scatter x4 -> x0, waiting for transfers between devices: 402 us -> none  [per_device(): lax.psum_scatter(part.reshape(rows * step, 2, -1), 'rows', scatter_dimens...]
    ppermute x24 -> x0, waiting for transfers between devices: 225 us -> none  [chain(): got = lax.ppermute(term, 'dp', pairs)]
    dot_general x8 -> x1, matrix products: 157 us -> 67.6 us  [fused(): jnp.einsum('tcb,tfc->tbf', gathered, weights, preferred_element_type=F32)]
    unnamed x4 -> x0, matrix products: 76.4 us -> none
    ppermute x24 -> x0, starting transfers between devices: 46 us -> none  [chain(): got = lax.ppermute(term, 'dp', pairs)]
    all_gather x4 -> x0, waiting for transfers between devices: 30.9 us -> none  [per_device(): piece = lax.all_gather(grad_pre, 'rows', axis=0)]
    convert_element_type x14 -> x4, other arithmetic: 29.1 us -> 2.67 us  [the longest x1 1.3 us: fused(): weight_valid = valid.astype(F32)]
  transfers between devices with their start and end apart: 32 -> 0, of which waited for: 17 -> 0; matrix products, arithmetic and copies ran while one was open for 25% -> 0% of each run, Pallas kernels for 0% -> 0%
where the time goes in v2:
time: 687 us; the launch traced here: 681 us
  Pallas kernels  486 us (71%)
  matrix products  67.6 us (10%)
  blocking collectives  56.4 us (8%)
  local copies, waits for them, and re-layouts  48.1 us (7%)
  other arithmetic  18.6 us (3%)
    pallas_call x1, Pallas kernels, fused(): pl.pallas_call(functools.partial(kernel, planes), out_shape=(jax.ShapeDty...  486 us
    dot_general x1, matrix products, fused(): jnp.einsum('tcb,tfc->tbf', gathered, weights, preferred_element_type=F32)  67.6 us
    psum x1, blocking collectives, fused(): totals = lax.psum(partial_value, ('dp', 'rows'))  40.9 us
    transpose x1, local copies, waits for them, and re-layouts, fused(): jnp.transpose(weights, (0, 2, 1)).reshape(towers, 4, 2, chunks, STEP, width)  24.8 us
    psum x1, blocking collectives, fused(): grad_bias, grad_stitch = lax.psum((grad_bias, grad_stitch), 'dp')  15.4 us

profile of v2, /device:TPU:8, one launch (start us, length us, event | category | flops | bytes accessed | tf_op | source)
XLA Modules:
  0.0 680.9 jit_solution(2613983911997233659)
XLA Ops:
  0.6 0.7 compare_convert_fusion
  1.3 1.3 copy.29.small_ref
  2.7 1.3 convert_element_type.27
  4.0 24.8 %copy.28 = bf16[2,4096,1152]{2,1,0:T(8,128)(2,1)} copy(bf16[2,4096,1152]{1,2,0:T(8,128)(2,1)} %bitcast.20) | data formatting | bytes 37748736 | tf_op jit(solution)/shard_map/transpose | solution.py:485
  28.8 1.9 reshape.162.stitch_ref
  30.7 1.1 reshape.161.bias_ref
  31.8 0.7 or_convert_fusion.pad_ref
  32.5 486.3 %towers.1 = (bf16[2,8,64,2048]{3,2,1,0:T(8,128)(2,1)}, bf16[2,2,2,2,8,64,2048]{6,5,4,3,2,1,0:T(8,128)(2,1)}, f32[2,2,8,64,1152]{4,3,2,1,0:T(8,128)}, f32[8,2,64,...) custom-call(bf16[2,2048,1152]{2,1,0:T(8,128)(2,1)} %x_hbm.1, ...), custom_call_target="tpu_custom_call" | custom-call | tf_op jit(solution)/shard_map/towers/pallas_call | solution.py:490
  518.8 1.5 slice_reduce_fusion.1
  520.4 1.4 multiply_subtract_fusion
  521.8 3.7 copy-done
  525.5 8.6 %fusion = f32[]{:T(128)} fusion(bf16[2,2048,1152]{2,1,0:T(8,128)(2,1)} %x_hbm.1, f32[2048]{0:T(1024)} %convert_element_type.27, f32[2048,1152]{1,0:T(8,128)S(1)} %multiply_subtract_fusion), kind=kLoop, calls=%fused_computation.1 | loop fusion | flops 23592960 | bytes 18882564 | tf_op jit(solution)/shard_map/reduce_sum | solution.py:562
  534.1 0.6 convert_reduce_fusion
  534.7 2.7 pad_maximum_fusion
  537.4 40.9 %psum.23 = f32[4]{0:T(128)S(1)} all-reduce(f32[4]{0:T(128)S(1)} %pad_maximum_fusion), channel_id=1, replica_groups=mesh['dp'=4,'rows'=8] {'dp','rows'}, use_global_device_ids=true, to_apply=%region_8.9 | all-reduce | flops 4 | bytes 32 | tf_op jit(solution)/shard_map/psum | solution.py:571
  578.3 0.6 fusion.13
  582.2 0.6 maximum_sqrt_fusion
  582.8 0.4 reduce_sum.55
  583.2 0.1 reshape.160
  583.3 0.2 reduce_sum.54
  583.6 15.4 %all-reduce = (f32[2,512]{1,0:T(2,128)}, f32[2,2,512]{2,1,0:T(2,128)}) all-reduce(f32[2,512]{1,0:T(2,128)S(1)} %reshape.159, f32[2,2,512]{2,1,0:T(2,128)S(1)} %reshape.160), channel_id=1, replica_groups=mesh['dp'=4,'rows'=8] {'dp'}, use_global_device_ids=true, to_apply=%region_1.2 | all-reduce | flops 3072 | bytes 24576 | tf_op jit(solution)/shard_map/psum | solution.py:570
  599.0 67.6 %multiply_convert_fusion = bf16[2,2048,1152]{2,1,0:T(8,128)(2,1)} fusion(bf16[2,4096,2048]{2,1,0:T(8,128)(2,1)} %bitcast.29, bf16[2,1152,4096]{2,1,0:T(8,128)(2,1)} %param.8, f32[2048,1152]{1,0:T(8,128)} %copy-done), kind=kOutput, calls=%fused_computation.2 | convolution fusion | flops 38664142848 | bytes 71303168 | tf_op jit(solution)/shard_map/tcb,tfc->tbf/dot_general | solution.py:556
  666.6 9.6 %copy.33 = f32[2,1024,1152]{1,2,0:T(8,128)} copy(f32[2,1024,1152]{2,1,0:T(8,128)} %bitcast.21) | data formatting | bytes 18874368 | tf_op jit(solution)/shard_map/reshape | solution.py:558
  676.1 4.8 copy.38
  (17 shorter events, 0.1 us)
Async XLA Ops:
  1.3 27.4 %copy-start.3 = (f32[2048]{0:T(1024)}, f32[2048]{0:T(1024)S(1)}, u32[]{:S(2)}) copy-start(f32[2048]{0:T(1024)S(1)} %compare_convert_fusion) | copy-start | bytes 24580
  4.0 24.8 %copy-start.5 = (f32[2,2,512]{2,1,0:T(2,128)S(1)}, f32[2,2,512]{2,1,0:T(2,128)}, u32[]{:S(2)}) copy-start(f32[2,2,512]{2,1,0:T(2,128)} %param.10) | copy-start | bytes 24580
  4.0 26.7 %copy-start.6 = (f32[2,512]{1,0:T(2,128)S(1)}, f32[2,512]{1,0:T(2,128)}, u32[]{:S(2)}) copy-start(f32[2,512]{1,0:T(2,128)} %param.9) | copy-start | bytes 12292
  518.8 15.3 %copy-start.4 = (s32[2048]{0:T(1024)S(1)}, s32[2048]{0:T(1024)}, u32[]{:S(2)}) copy-start(s32[2048]{0:T(1024)} %param.12) | copy-start | bytes 24580
  518.8 64.0 %copy-start.1 = (f32[8,2,2,64,128]{4,3,2,1,0:T(8,128)S(1)}, f32[8,2,2,64,128]{4,3,2,1,0:T(8,128)}, u32[]{:S(2)}) copy-start(f32[8,2,2,64,128]{4,3,2,1,0:T(8,128)} %get-tuple-element.16) | copy-start | bytes 3145732
  518.8 64.4 %copy-start.2 = (f32[8,2,64,128]{3,2,1,0:T(8,128)S(1)}, f32[8,2,64,128]{3,2,1,0:T(8,128)}, u32[]{:S(2)}) copy-start(f32[8,2,64,128]{3,2,1,0:T(8,128)} %get-tuple-element.15) | copy-start | bytes 1572868
  521.8 3.7 copy-start

commit v3 on v2

--- a/solution.py
+++ b/solution.py
@@ -22,25 +22,33 @@
     return sum(value[:, i : i + 128] for i in range(0, value.shape[1], 128))
 
 
+def lane_sums(value):
+    ones = jnp.ones((8, 128), F32)
+    return lax.dot_general(
+        ones, value, (((1,), (1,)), ((), ())), precision=lax.Precision.HIGHEST, preferred_element_type=F32
+    )
+
+
 def kernel(
     planes,
     x_hbm,
-    wt_hbm,
+    w_hbm,
     cot_hbm,
+    image_ref,
+    pad_row_ref,
+    pad_col_ref,
+    valid_ref,
     small_ref,
-    pad_ref,
-    valid_ref,
-    bias_ref,
-    stitch_ref,
+    mix_ref,
     st_hbm,
+    gx_hbm,
+    gw_hbm,
+    stats_ref,
     g_hbm,
-    gw_hbm,
-    gb_ref,
-    gs_ref,
-    sq_ref,
+    acc_hbm,
     xb,
-    wo,
-    wp,
+    raw,
+    wt,
     part,
     r1,
     r2,
@@ -51,6 +59,17 @@
     zsend,
     zrecv,
     zfin,
+    gb_ref,
+    gs_ref,
+    sq_ref,
+    usq_ref,
+    wgx,
+    gtile,
+    acc,
+    gout,
+    scur,
+    srecv,
+    stats,
     x_sem,
     xs_sem,
     xr_sem,
@@ -73,12 +92,26 @@
     z_s,
     z_r,
     zf_sem,
+    z_free,
+    wg_sem,
+    gt_sem,
+    ai_sem,
+    ao_sem,
+    go_sem,
+    sc_s,
+    sc_r,
+    zs_s,
+    zs_r,
 ):
     towers, images, width = x_hbm.shape
     chunks = cot_hbm.shape[1]
+    pairs = chunks // 2
+    mine = chunks * STEP
     per_chunk = images // IMAGES
     total = chunks * per_chunk
+    tiles = towers * per_chunk
     last = planes - 1
+    halves = 8 // planes
 
     z = lax.axis_index("dp")
     row = lax.axis_index("rows")
@@ -93,14 +126,8 @@
     barrier = pltpu.get_barrier_semaphore()
     for there in (to_x, to_y, to_core):
         pl.semaphore_signal(barrier, inc=1, device_id=there, device_id_type=MESH)
-
-    @pl.when(z > 0)
-    def _():
-        pl.semaphore_signal(barrier, inc=1, device_id=(z - 1, row), device_id_type=MESH)
-
-    @pl.when(z < last)
-    def _():
-        pl.semaphore_signal(barrier, inc=1, device_id=(z + 1, row), device_id_type=MESH)
+    for off in range(1, planes):
+        pl.semaphore_signal(barrier, inc=1, device_id=((z + off) % planes, row), device_id_type=MESH)
 
     def remote(src, dst, send, recv, there):
         return pltpu.make_async_remote_copy(
@@ -118,11 +145,22 @@
         cut = pl.ds(i * IMAGES, IMAGES)
         return remote(x_hbm.at[:, cut], xb.at[1, :, cut], xs_sem.at[i], xr_sem.at[i], to_core)
 
-    def w_local(k):
-        return pltpu.make_async_copy(wt_hbm.at[:, :, core, k], wo.at[k % 2], wo_sem.at[k % 2])
-
-    def w_remote(k):
-        return remote(wt_hbm.at[:, :, oc, k], wp.at[k], ws_sem.at[k], wr_sem.at[k], to_core)
+    def w_lanes(owner, p):
+        return pl.ds(pl.multiple_of(owner * mine + p * 2 * STEP, 2 * STEP), 2 * STEP)
+
+    def w_local(p):
+        return [
+            pltpu.make_async_copy(w_hbm.at[:, :, w_lanes(c * 2 + core, p)], raw.at[0, :, c], wo_sem.at[c])
+            for c in range(4)
+        ]
+
+    def w_remote(p):
+        return [
+            remote(
+                w_hbm.at[:, :, w_lanes(c * 2 + oc, p)], raw.at[1, :, c], ws_sem.at[c], wr_sem.at[c], to_core
+            )
+            for c in range(4)
+        ]
 
     def rs1(q):
         s = q % SLOTS
@@ -175,13 +213,45 @@
     def gw_copy(k):
         return pltpu.make_async_copy(zfin, gw_hbm.at[:, :, k], zf_sem)
 
-    def z_slot(k, j):
-        return j if j < planes - 2 else j + k % 2
-
     def z_copy(k, j, way):
-        n = z_slot(k, j)
         there = (z + 1, row) if way == 0 else (z - 1, row)
-        return remote(zsend.at[way, j], zrecv.at[way, n], z_s.at[way, j], z_r.at[way, n], there)
+        return remote(zsend.at[way, j], zrecv.at[way, j], z_s.at[way, j], z_r.at[way, j], there)
+
+    def wg_load(g):
+        p, t = g // tiles, (g % tiles) // per_chunk
+        return [
+            pltpu.make_async_copy(w_hbm.at[t, :, w_lanes(r, p)], wgx.at[:, pl.ds(r * 128, 128)], wg_sem.at[r])
+            for r in range(8)
+        ]
+
+    def g_load(g):
+        p, t, i = g // tiles, (g % tiles) // per_chunk, g % per_chunk
+        return pltpu.make_async_copy(
+            g_hbm.at[t, :, :, :, pl.ds(p * 2, 2), :, lanes(i)], gtile.at[g % 2], gt_sem.at[g % 2]
+        )
+
+    def acc_in(g):
+        return pltpu.make_async_copy(acc_hbm.at[g % tiles], acc.at[g % 2], ai_sem.at[g % 2])
+
+    def acc_out(g):
+        return pltpu.make_async_copy(acc.at[g % 2], acc_hbm.at[g % tiles], ao_sem.at[g % 2])
+
+    def gx_out(g):
+        t = (g % tiles) // per_chunk
+        return pltpu.make_async_copy(gout.at[g % 2], gx_hbm.at[t, :, lanes(g)], go_sem.at[g % 2])
+
+    def in_plane(n):
+        there = (to_x, to_y, to_core)[n]
+        return remote(scur.at[n], srecv.at[n], sc_s.at[n], sc_r.at[n], there)
+
+    def to_plane(off):
+        there = ((z + off) % planes, row)
+        return remote(stats.at[z], stats.at[z], zs_s.at[off - 1], zs_r.at[off - 1], there)
+
+    def from_plane(off):
+        there = ((z + off) % planes, row)
+        held = stats.at[(z + planes - off) % planes]
+        return remote(held, held, zs_s.at[off - 1], zs_r.at[off - 1], there)
 
     def start(copies):
         for c in copies:
@@ -206,19 +276,41 @@
             work(q)
             start(sends(q))
 
+    def turn(p):
+        for c in w_local(p):
+            c.wait()
+        wait_recv(w_remote(p))
+
+        def one(n, carry):
+            side, t, c = n // 8, (n // 4) % 2, n % 4
+            turned = jnp.transpose(raw[side, t, c])
+            wt[side, t, 0, c] = turned[:STEP]
+            wt[side, t, 1, c] = turned[STEP:]
+            return carry
+
+        lax.fori_loop(0, 16, one, 0)
+
+        @pl.when(p + 1 < pairs)
+        def _():
+            start(w_local(p + 1))
+
     def forward(q):
         k, i, s = q // per_chunk, q % per_chunk, q % SLOTS
+        p, h = k // 2, k % 2
 
         cot_copy(q).start()
 
-        @pl.when(i == 0)
-        def _():
-            w_local(k).wait()
-            w_remote(k).wait_recv()
-
-            @pl.when(k + 1 < chunks)
+        @pl.when((i == 0) & (h == 0))
+        def _():
+            turn(p)
+
+        @pl.when((i == 0) & (h == 1))
+        def _():
+            wait_send(w_remote(p))
+
+            @pl.when(p + 1 < pairs)
             def _():
-                w_local(k + 1).start()
+                start(w_remote(p + 1))
 
         cut = pl.ds(pl.multiple_of(i * IMAGES, IMAGES), IMAGES)
 
@@ -226,19 +318,23 @@
         def _():
             x_local(i).wait()
             x_remote(i).wait_recv()
-            keep = (1.0 - small_ref[cut, :] * pad_ref[...]).astype(BF16)
-            for side in range(2):
-                for t in range(towers):
-                    xb[side, t, cut] = xb[side, t, cut] * keep
+            keep = (1.0 - image_ref[cut, 0:1] * pad_row_ref[...]).astype(BF16)
+            valid = image_ref[cut, 1:2]
+            for t in range(towers):
+                used = xb[0, t, cut] * keep
+                xb[0, t, cut] = used
+                used = used.astype(F32)
+                usq_ref[...] = usq_ref[...] + jnp.sum(used * used * valid, axis=0, keepdims=True)
+                xb[1, t, cut] = xb[1, t, cut] * keep
 
         for t in range(towers):
             out = lax.dot_general(
-                wo[k % 2, t].reshape(4 * STEP, width),
+                wt[0, t, h].reshape(4 * STEP, width),
                 xb[0, t, cut],
                 (((1,), (1,)), ((), ())),
                 preferred_element_type=F32,
             ) + lax.dot_general(
-                wp[k, t].reshape(4 * STEP, width),
+                wt[1, t, h].reshape(4 * STEP, width),
                 xb[1, t, cut],
                 (((1,), (1,)), ((), ())),
                 preferred_element_type=F32,
@@ -266,19 +362,22 @@
             st_copy(q - SLOTS).wait()
 
         valid = valid_ref[i]
-        pre = [part[s, y, x, t] + r2[s, t] + bias_ref[t, k] for t in range(2)]
+        mix = mix_ref[k]
+        bias = [mix[:, t : t + 1] for t in range(2)]
+        stitch = [[mix[:, 2 + 2 * a + b : 3 + 2 * a + b] for b in range(2)] for a in range(2)]
+        pre = [part[s, y, x, t] + r2[s, t] + bias[t] for t in range(2)]
         act = [jnp.maximum(p, 0.0) for p in pre]
         up = [cbuf[s, t].astype(F32) * valid for t in range(2)]
         cut = lanes(q)
         for a in range(2):
-            out = stitch_ref[a, 0, k] * act[0] + stitch_ref[a, 1, k] * act[1]
+            out = stitch[a][0] * act[0] + stitch[a][1] * act[1]
             stbuf[s, a] = out.astype(BF16)
             sq_ref[1] = sq_ref[1] + fold(out * out * valid)
             for b in range(2):
                 gs_ref[k, a, b] = gs_ref[k, a, b] + fold(up[a] * act[b])
         for t in range(2):
             sq_ref[0] = sq_ref[0] + fold(pre[t] * pre[t] * valid)
-            grad = stitch_ref[0, t, k] * up[0] + stitch_ref[1, t, k] * up[1]
+            grad = stitch[0][t] * up[0] + stitch[1][t] * up[1]
             grad = jnp.where(pre[t] > 0, grad, 0.0).astype(BF16)
             gfull[k % 2, t, y, x, core, :, cut] = grad
             gb_ref[k, t] = gb_ref[k, t] + fold(grad.astype(F32))
@@ -298,61 +397,12 @@
                 xb[0, t, :, n * third : (n + 1) * third],
                 preferred_element_type=F32,
             )
-            value = value.astype(BF16).reshape(planes, 8 // planes, STEP, third)
+            value = value.astype(BF16).reshape(planes, halves, STEP, third)
             for d in range(planes):
-                for e in range(8 // planes):
+                for e in range(halves):
                     zo[t, d, e, :, n * third : (n + 1) * third] = value[d, e]
 
-    halves = 8 // planes
-
     def chain(k, j):
-        for way in range(2):
-            near = z if way == 0 else last - z
-            got = z_copy(k, j - 1, way) if j > 0 else None
-            if j > 0:
-
-                @pl.when((near >= 1) & (near <= j))
-                def _():
-                    got.wait_recv()
-
-            if j <= planes - 2:
-
-                @pl.when(near <= j)
-                def _():
-                    dest = last - j + z if way == 0 else j - last + z
-
-                    @pl.when(k > 0)
-                    def _():
-                        z_copy(k - 1, j, way).wait_send()
-
-                    if j > 0:
-                        n = z_slot(k, j - 1)
-
-                        @pl.when(near >= 1)
-                        def _():
-                            def add(i, carry):
-                                t, e = i // halves, i % halves
-                                value = zo[t, dest, e].astype(F32) + zrecv[way, n, t, e].astype(F32)
-                                zsend[way, j, t, e] = value.astype(BF16)
-                                return carry
-
-                            lax.fori_loop(0, towers * halves, add, 0)
-
-                        @pl.when(near == 0)
-                        def _():
-                            zsend[way, j] = zo[:, dest]
-
-                    else:
-                        zsend[way, j] = zo[:, dest]
-
-        for way in range(2):
-            near = z if way == 0 else last - z
-            if j <= planes - 2:
-
-                @pl.when(near <= j)
-                def _():
-                    z_copy(k, j, way).start()
-
         if j == planes - 2:
 
             @pl.when(k > 0)
@@ -365,47 +415,166 @@
                 return carry
 
             lax.fori_loop(0, towers * halves, begin, 0)
-        if j == planes - 1:
-            n = z_slot(k, j - 1)
-            for way in range(2):
-                near = z if way == 0 else last - z
+        for way in range(2):
+            near = z if way == 0 else last - z
+            source = (z - 1, row) if way == 0 else (z + 1, row)
+
+            def freed():
+                @pl.when(k + 1 < chunks)
+                def _():
+                    pl.semaphore_signal(
+                        z_free.at[way, j - 1], inc=1, device_id=source, device_id_type=MESH
+                    )
+
+            if j <= planes - 2:
+
+                @pl.when(near <= j)
+                def _():
+                    dest = last - j + z if way == 0 else j - last + z
+
+                    @pl.when(k > 0)
+                    def _():
+                        z_copy(k - 1, j, way).wait_send()
+
+                    if j > 0:
+
+                        @pl.when(near >= 1)
+                        def _():
+                            z_copy(k, j - 1, way).wait_recv()
+
+                            def add(i, carry):
+                                t, e = i // halves, i % halves
+                                value = zo[t, dest, e].astype(F32) + zrecv[way, j - 1, t, e].astype(F32)
+                                zsend[way, j, t, e] = value.astype(BF16)
+                                return carry
+
+                            lax.fori_loop(0, towers * halves, add, 0)
+                            freed()
+
+                        @pl.when(near == 0)
+                        def _():
+                            zsend[way, j] = zo[:, dest]
+
+                    else:
+                        zsend[way, j] = zo[:, dest]
+
+                    @pl.when(k > 0)
+                    def _():
+                        pl.semaphore_wait(z_free.at[way, j], 1)
+
+                    z_copy(k, j, way).start()
+
+            else:
 
                 @pl.when(near >= 1)
                 def _():
+                    z_copy(k, j - 1, way).wait_recv()
+
                     def more(i, carry):
                         t, e = i // halves, i % halves
-                        zfin[t, e] = zfin[t, e] + zrecv[way, n, t, e].astype(F32)
+                        zfin[t, e] = zfin[t, e] + zrecv[way, j - 1, t, e].astype(F32)
                         return carry
 
                     lax.fori_loop(0, towers * halves, more, 0)
-
+                    freed()
+
+        if j == planes - 1:
             gw_copy(k).start()
 
-    x_local(0).start()
-    w_local(0).start()
-    for i in range(1, per_chunk):
+    def prepare(g):
+        g_load(g).start()
+
+        @pl.when(g % per_chunk == 0)
+        def _():
+            start(wg_load(g))
+
+        @pl.when((g >= 2) & (g - 2 < (pairs - 1) * tiles))
+        def _():
+            acc_out(g - 2).wait()
+
+        @pl.when(g >= tiles)
+        def _():
+            acc_in(g).start()
+
+    def tile(g):
+        g_load(g).wait()
+
+        @pl.when(g % per_chunk == 0)
+        def _():
+            for c in wg_load(g):
+                c.wait()
+
+        value = jnp.dot(
+            wgx[...], gtile[g % 2].reshape(16 * STEP, IMAGES), preferred_element_type=F32
+        )
+
+        @pl.when(g < tiles)
+        def _():
+            acc[g % 2] = value
+
+        @pl.when(g >= tiles)
+        def _():
+            acc_in(g).wait()
+            acc[g % 2] = acc[g % 2] + value
+
+        @pl.when(g < (pairs - 1) * tiles)
+        def _():
+            acc_out(g).start()
+
+        @pl.when(g >= (pairs - 1) * tiles)
+        def _():
+            @pl.when(g >= (pairs - 1) * tiles + 2)
+            def _():
+                gx_out(g - 2).wait()
+
+            keep = 1.0 - pad_col_ref[...] * small_ref[g % per_chunk]
+            gout[g % 2] = (acc[g % 2] * keep).astype(BF16)
+            gx_out(g).start()
+
+    def sums(n):
+        if n == 0:
+            scur[0] = jnp.zeros_like(scur[0])
+            scur[0, 0:1] = fold(usq_ref[...])
+            scur[0, 1:2] = jnp.sum(sq_ref[0], axis=0, keepdims=True)
+            scur[0, 2:3] = jnp.sum(sq_ref[1], axis=0, keepdims=True)
+            scur[0, 3:4] = fold(sum(valid_ref[i] for i in range(per_chunk)))
+            for k in range(chunks):
+                at = k * 6 * STEP
+                stats[z, :, at : at + 2 * STEP] = lane_sums(gb_ref[k].reshape(2 * STEP, 128))
+                stats[z, :, at + 2 * STEP : at + 6 * STEP] = lane_sums(gs_ref[k].reshape(4 * STEP, 128))
+        else:
+            in_plane(n - 1).wait()
+            value = scur[n - 1] + srecv[n - 1]
+            if n < 3:
+                scur[n] = value
+            else:
+                stats[z, :, chunks * 6 * STEP :] = value
+        if n < 3:
+            in_plane(n).start()
+        else:
+            for off in range(1, planes):
+                to_plane(off).start()
+
+    start(w_local(0))
+    for i in range(per_chunk):
         x_local(i).start()
-    pl.semaphore_wait(barrier, 3 + jnp.minimum(z, 1) + jnp.minimum(last - z, 1))
-    w_remote(0).start()
+    pl.semaphore_wait(barrier, 2 + planes)
+    start(w_remote(0))
 
     def send_x(i, carry):
         x_remote(i).start()
         return carry
 
     lax.fori_loop(0, per_chunk, send_x, 0)
-
-    def send_w(k, carry):
-        w_remote(k).start()
-        return carry
-
-    lax.fori_loop(1, chunks, send_w, 0)
     gb_ref[...] = jnp.zeros_like(gb_ref)
     gs_ref[...] = jnp.zeros_like(gs_ref)
     sq_ref[...] = jnp.zeros_like(sq_ref)
+    usq_ref[...] = jnp.zeros_like(usq_ref)
 
     ready = per_chunk - 1 + 5
-    space = per_chunk // 4
-    offsets = [2 + j * space for j in range(planes)]
+    offsets = [2 + 3 * j for j in range(planes)]
+    ends = [2 + 5 * j for j in range(planes)]
+    first = per_chunk + 3
 
     def body(s, carry):
         stage(s, forward, rs1, rs1, rs2)
@@ -418,12 +587,29 @@
         def _():
             wait_recv(cx(s - 5))
 
+        for n in range(4):
+
+            @pl.when(s == total + 2 + n)
+            def _():
+                sums(n)
+
         @pl.when(s >= ready)
         def _():
             done = s - ready
             k = done // per_chunk
             at = done % per_chunk
 
+            def step(j):
+                since = done - offsets[j]
+                usual = (since >= 0) & (since % per_chunk == 0) & (since // per_chunk < chunks - 1)
+                final = done == (chunks - 1) * per_chunk + ends[j]
+
+                @pl.when(usual | final)
+                def _():
+                    chain(jnp.where(final, chunks - 1, since // per_chunk), j)
+
+            for j in range(1, planes):
+                step(j)
             for n in range(3):
 
                 @pl.when((at == n) & (k < chunks))
@@ -434,15 +620,20 @@
                     if n == 2:
                         g_copy(k).wait()
 
-            for j, off in enumerate(offsets):
-
-                @pl.when((done >= off) & ((done - off) % per_chunk == 0) & ((done - off) // per_chunk < chunks))
-                def _():
-                    chain((done - off) // per_chunk, j)
+            step(0)
+            g = done - first
+
+            @pl.when((g >= 0) & (g < pairs * tiles))
+            def _():
+                tile(g)
+
+            @pl.when((g >= -1) & (g < pairs * tiles - 1))
+            def _():
+                prepare(g + 1)
 
         return carry
 
-    lax.fori_loop(0, total + ready - per_chunk + 1 + offsets[-1] + 1, body, 0)
+    lax.fori_loop(0, ready + max((chunks - 1) * per_chunk + ends[-1], first + pairs * tiles - 1) + 1, body, 0)
 
     def drain(q, carry):
         st_copy(q).wait()
@@ -455,12 +646,8 @@
         return carry
 
     lax.fori_loop(0, per_chunk, drain_x, 0)
-
-    def drain_w(k, carry):
-        w_remote(k).wait_send()
-        return carry
-
-    lax.fori_loop(0, chunks, drain_w, 0)
+    for g in (pairs * tiles - 2, pairs * tiles - 1):
+        gx_out(g).wait()
     gw_copy(chunks - 1).wait()
     for way in range(2):
         near = z if way == 0 else last - z
@@ -469,6 +656,11 @@
             @pl.when(near <= j)
             def _():
                 z_copy(chunks - 1, j, way).wait_send()
+
+    for off in range(1, planes):
+        to_plane(off).wait_send()
+        from_plane(off).wait_recv()
+    stats_ref[...] = sum(stats[d] for d in range(planes))
 
 
 def fused(inputs, weights, bias, stitch, cotangent, valid, size_class):
@@ -478,31 +670,32 @@
     chunks = mine // STEP
     per_chunk = images // IMAGES
     halves = 8 // planes
-    small = (size_class == 195).astype(F32)[:, None]
+    tiles = towers * per_chunk
+    small = (size_class == 195).astype(F32)
     place = lax.iota(jnp.int32, width) % 36
-    padded = ((place // 6 == 5) | (place % 6 == 5)).astype(F32)[None, :]
+    padded = ((place // 6 == 5) | (place % 6 == 5)).astype(F32)
     weight_valid = valid.astype(F32)
-    turned = jnp.transpose(weights, (0, 2, 1)).reshape(towers, 4, 2, chunks, STEP, width)
+    mix = jnp.concatenate([bias, stitch.reshape(4, mine)], axis=0).reshape(6, chunks, STEP)
+    many = chunks * 6 * STEP + 128
     vmem = pl.BlockSpec(memory_space=pltpu.VMEM)
     hbm = pl.BlockSpec(memory_space=pl.ANY)
     dma = pltpu.SemaphoreType.DMA
-    zslots = planes
-    outs = pl.pallas_call(
+    stitched, grad_inputs, grad_weights, stats, _, _ = pl.pallas_call(
         functools.partial(kernel, planes),
         out_shape=(
             jax.ShapeDtypeStruct((2, chunks, STEP, images), BF16),
+            jax.ShapeDtypeStruct((towers, width, images), BF16),
+            jax.ShapeDtypeStruct((2, halves, chunks, STEP, width), F32),
+            jax.ShapeDtypeStruct((8, many), F32),
             jax.ShapeDtypeStruct((2, 2, 2, 2, chunks, STEP, images), BF16),
-            jax.ShapeDtypeStruct((2, halves, chunks, STEP, width), F32),
-            jax.ShapeDtypeStruct((chunks, 2, STEP, 128), F32),
-            jax.ShapeDtypeStruct((chunks, 2, 2, STEP, 128), F32),
-            jax.ShapeDtypeStruct((2, STEP, 128), F32),
+            jax.ShapeDtypeStruct((tiles, width, IMAGES), F32),
         ),
-        in_specs=[hbm] * 3 + [vmem] * 5,
-        out_specs=(hbm, hbm, hbm, vmem, vmem, vmem),
+        in_specs=[hbm] * 3 + [vmem] * 6,
+        out_specs=(hbm, hbm, hbm, vmem, hbm, hbm),
         scratch_shapes=[
             pltpu.VMEM((2, towers, images, width), BF16),
-            pltpu.VMEM((2, towers, 4, STEP, width), BF16),
-            pltpu.VMEM((chunks, towers, 4, STEP, width), BF16),
+            pltpu.VMEM((2, towers, 4, width, 2 * STEP), BF16),
+            pltpu.VMEM((2, towers, 2, 4, STEP, width), BF16),
             pltpu.VMEM((SLOTS, 2, 2, towers, STEP, IMAGES), F32),
             pltpu.VMEM((SLOTS, 2, 2, STEP, IMAGES), F32),
             pltpu.VMEM((SLOTS, 2, STEP, IMAGES), F32),
@@ -511,14 +704,25 @@
             pltpu.VMEM((SLOTS, 2, STEP, IMAGES), BF16),
             pltpu.VMEM((towers, planes, halves, STEP, width), BF16),
             pltpu.VMEM((2, planes - 1, towers, halves, STEP, width), BF16),
-            pltpu.VMEM((2, zslots, towers, halves, STEP, width), BF16),
+            pltpu.VMEM((2, planes - 1, towers, halves, STEP, width), BF16),
             pltpu.VMEM((towers, halves, STEP, width), F32),
+            pltpu.VMEM((chunks, 2, STEP, 128), F32),
+            pltpu.VMEM((chunks, 2, 2, STEP, 128), F32),
+            pltpu.VMEM((2, STEP, 128), F32),
+            pltpu.VMEM((1, width), F32),
+            pltpu.VMEM((width, 16 * STEP), BF16),
+            pltpu.VMEM((2, 2, 2, 2, 2, STEP, IMAGES), BF16),
+            pltpu.VMEM((2, width, IMAGES), F32),
+            pltpu.VMEM((2, width, IMAGES), BF16),
+            pltpu.VMEM((3, 8, 128), F32),
+            pltpu.VMEM((3, 8, 128), F32),
+            pltpu.VMEM((planes, 8, many), F32),
             dma((per_chunk,)),
             dma((per_chunk,)),
             dma((per_chunk,)),
-            dma((2,)),
-            dma((chunks,)),
-            dma((chunks,)),
+            dma((4,)),
+            dma((4,)),
+            dma((4,)),
             dma((SLOTS, 2)),
             dma((SLOTS, 2)),
             dma((SLOTS, 2)),
@@ -533,8 +737,18 @@
             dma((SLOTS,)),
             dma((2,)),
             dma((2, planes - 1)),
-            dma((2, zslots)),
+            dma((2, planes - 1)),
             dma,
+            pltpu.SemaphoreType.REGULAR((2, planes - 1)),
+            dma((8,)),
+            dma((2,)),
+            dma((2,)),
+            dma((2,)),
+            dma((2,)),
+            dma((3,)),
+            dma((3,)),
+            dma((planes - 1,)),
+            dma((planes - 1,)),
         ],
         compiler_params=pltpu.CompilerParams(
             collective_id=0, has_side_effects=True, vmem_limit_bytes=67043328
@@ -542,40 +756,24 @@
         name="towers",
     )(
         inputs,
-        turned,
+        weights,
         cotangent.reshape(2, chunks, STEP, images),
-        small,
-        padded,
+        jnp.stack([small, weight_valid], axis=1),
+        padded[None, :],
+        padded[:, None],
         weight_valid.reshape(per_chunk, 1, IMAGES),
-        bias.reshape(2, chunks, STEP, 1),
-        stitch.reshape(2, 2, chunks, STEP, 1),
+        small.reshape(per_chunk, 1, IMAGES),
+        jnp.transpose(mix, (1, 2, 0)),
     )
-    stitched, gathered, grad_weights, grad_bias, grad_stitch, squares = outs
-    keep = 1.0 - small * padded
-    gathered = gathered.reshape(towers, -1, images)
-    total_x = jnp.einsum("tcb,tfc->tbf", gathered, weights, preferred_element_type=F32)
-    grad_inputs = (total_x * keep[None]).astype(BF16)
     grad_weights = jnp.transpose(grad_weights.reshape(towers, -1, width), (0, 2, 1))
-    used_wide = inputs.astype(F32) * keep[None]
-    partial_value = jnp.stack(
-        [
-            jnp.sum(weight_valid[None, :, None] * used_wide * used_wide),
-            jnp.sum(squares[0]),
-            jnp.sum(squares[1]),
-            jnp.sum(weight_valid),
-        ]
-    )
-    grad_bias = jnp.transpose(jnp.sum(grad_bias, axis=3), (1, 0, 2)).reshape(2, mine)
-    grad_stitch = jnp.transpose(jnp.sum(grad_stitch, axis=4), (1, 2, 0, 3)).reshape(2, 2, mine)
-    grad_bias, grad_stitch = lax.psum((grad_bias, grad_stitch), "dp")
-    totals = lax.psum(partial_value, ("dp", "rows"))
+    grads = jnp.transpose(stats[0, :-128].reshape(chunks, 6, STEP), (1, 0, 2)).reshape(6, mine)
     return (
         stitched.reshape(2, mine, images),
-        grad_inputs,
+        jnp.transpose(grad_inputs, (0, 2, 1)),
         grad_weights,
-        grad_bias,
-        grad_stitch,
-        rms(totals),
+        grads[:2],
+        grads[2:].reshape(2, 2, mine),
+        rms(jnp.sum(stats[:4, -128:], axis=1)),
     )
 
 

time: 687 us -> 544 us (0.79)
  matrix products: 67.6 us -> 0 us
  blocking collectives: 56.4 us -> 0 us
  local copies, waits for them, and re-layouts: 48.1 us -> 33.7 us
  other arithmetic: 18.6 us -> 5.11 us
  Pallas kernels: 486 us -> 498 us
    dot_general x1 -> x0, matrix products: 67.6 us -> none  [fused(): jnp.einsum('tcb,tfc->tbf', gathered, weights, preferred_element_type=F32)]
    psum x2 -> x0, blocking collectives: 56.4 us -> none  [the longest x1 40.9 us: fused(): totals = lax.psum(partial_value, ('dp', 'rows'))]
    transpose x3 -> x0, local copies, waits for them, and re-layouts: 24.8 us -> none  [the longest x1 24.8 us: fused(): jnp.transpose(weights, (0, 2, 1)).reshape(towers, 4, 2, chunks, STEP, width)]
    pallas_call x1, Pallas kernels: 486 us -> 498 us  [fused(): pl.pallas_call(functools.partial(kernel, planes), out_shape=(jax.ShapeDty...]
    reduce_sum x5 -> x1, other arithmetic: 11.3 us -> 0.79 us  [fused(): jnp.sum(stats[:4, -128:], axis=1)]
    unnamed x15 -> x6, local copies, waits for them, and re-layouts: 8.55 us -> 17.4 us
where the time goes in v3:
time: 544 us; the launch traced here: 541 us
  Pallas kernels  498 us (92%)
  local copies, waits for them, and re-layouts  33.7 us (6%)
    pallas_call x1, Pallas kernels, fused(): pl.pallas_call(functools.partial(kernel, planes), out_shape=(jax.ShapeDty...  498 us
    unnamed x6, local copies, waits for them, and re-layouts  17.4 us

profile of v3, /device:TPU:8, one launch (start us, length us, event | category | flops | bytes accessed | tf_op | source)
XLA Modules:
  0.0 540.6 jit_solution(11987482969110035122)
XLA Ops:
  0.6 0.7 or_convert_fusion.pad_row_ref
  1.3 0.7 convert_element_type.26
  2.0 0.0 copy-start
  2.0 0.7 compare_convert_fusion
  2.7 0.0 copy-start.1
  2.7 0.8 concatenate.8
  3.5 0.0 copy-done
  3.5 0.0 copy-done.1
  3.5 0.8 concatenate.9
  4.3 0.9 copy.41
  5.2 1.6 fusion.11.pad_col_ref
  6.8 1.3 copy.42.image_ref
  8.1 497.9 %towers.1 = (bf16[2,8,64,2048]{3,2,1,0:T(8,128)(2,1)}, bf16[2,1152,2048]{2,1,0:T(8,128)(2,1)}, f32[2,2,8,64,1152]{4,3,2,1,0:T(8,128)}, f32[8,3200]{1,0:T(8,128)}...) custom-call(bf16[2,2048,1152]{2,1,0:T(8,128)(2,1)} %x_hbm.1, bf16[2,1152,4096]{2,1,0:T(8,128)(2,1)} %w_hbm.1, ...), custom_call_target="tpu_custom_call" | custom-call | tf_op jit(solution)/shard_map/towers/pallas_call | solution.py:683
  506.0 12.6 %copy.46 = bf16[2,2048,1152]{2,1,0:T(8,128)(2,1)} copy(bf16[2,2048,1152]{1,2,0:T(8,128)(2,1)} %bitcast.13) | data formatting | bytes 18874368
  518.6 0.8 slice_reduce_fusion.1
  519.4 0.9 slice_reduce_fusion
  520.4 0.6 fusion.12
  524.2 0.6 maximum_sqrt_fusion
  524.8 0.1 reshape_squeeze.3
  524.9 0.7 reshape.194
  525.6 0.7 slice.30
  526.2 9.6 %copy.43 = f32[2,1024,1152]{1,2,0:T(8,128)} copy(f32[2,1024,1152]{2,1,0:T(8,128)} %bitcast.11) | data formatting | bytes 18874368 | tf_op jit(solution)/shard_map/reshape | solution.py:768
  535.8 4.8 copy.48
  (6 shorter events, 0.0 us)
Async XLA Ops:
  2.0 1.5 copy-start
  2.7 0.8 copy-start.1

commit v4 on v3

--- a/solution.py
+++ b/solution.py
@@ -13,6 +13,8 @@
 STEP = 64
 IMAGES = 256
 SLOTS = 4
+WORDS = 40
+TOP = 2.0**18 - 2.0
 F32 = jnp.float32
 BF16 = jnp.bfloat16
 MESH = pl.DeviceIdType.MESH
@@ -27,6 +29,37 @@
     return lax.dot_general(
         ones, value, (((1,), (1,)), ((), ())), precision=lax.Precision.HIGHEST, preferred_element_type=F32
     )
+
+
+def pack(value):
+    tiles = [value[8 * i : 8 * i + 8] for i in range(8)]
+    top = jnp.abs(tiles[0])
+    for v in tiles[1:]:
+        top = jnp.maximum(top, jnp.abs(v))
+    exponent = jnp.floor(jnp.log2(jnp.maximum(top, 2.0**-60))) + 1.0
+    scale = jnp.exp2(-exponent) * TOP
+    q = [jnp.round(v * scale).astype(jnp.int32) for v in tiles]
+    low = [v & 0x1FFF for v in q[5:]]
+    high = [(v >> 13) & 0x3F for v in q[5:]]
+    words = [
+        (q[0] << 13) | low[0],
+        (q[1] << 13) | low[1],
+        (q[2] << 13) | low[2],
+        (q[3] << 13) | high[0] | (high[1] << 6),
+        (q[4] << 13) | high[2] | ((exponent.astype(jnp.int32) & 0x7F) << 6),
+    ]
+    return jnp.concatenate(words, axis=0)
+
+
+def unpack(words):
+    w = [words[8 * i : 8 * i + 8] for i in range(5)]
+    exponent = (w[4] << 19) >> 25
+    scale = jnp.exp2(exponent.astype(F32)) * (1.0 / TOP)
+    q = [v >> 13 for v in w]
+    q.append(((w[3] << 26) >> 26 << 13) | (w[0] & 0x1FFF))
+    q.append(((w[3] << 20) >> 26 << 13) | (w[1] & 0x1FFF))
+    q.append(((w[4] << 26) >> 26 << 13) | (w[2] & 0x1FFF))
+    return jnp.concatenate([v.astype(F32) * scale for v in q], axis=0)
 
 
 def kernel(
@@ -36,9 +69,7 @@
     cot_hbm,
     image_ref,
     pad_row_ref,
-    pad_col_ref,
     valid_ref,
-    small_ref,
     mix_ref,
     st_hbm,
     gx_hbm,
@@ -50,6 +81,8 @@
     raw,
     wt,
     part,
+    p1,
+    p2,
     r1,
     r2,
     gfull,
@@ -165,15 +198,15 @@
     def rs1(q):
         s = q % SLOTS
         return (
-            remote(part.at[s, :, ox, 0], r1.at[s, 0], rs1_s.at[s, 0], rs1_r.at[s, 0], to_x),
-            remote(part.at[s, oy, :, 1], r1.at[s, 1], rs1_s.at[s, 1], rs1_r.at[s, 1], to_y),
+            remote(p1.at[s, 0], r1.at[s, 0], rs1_s.at[s, 0], rs1_r.at[s, 0], to_x),
+            remote(p1.at[s, 1], r1.at[s, 1], rs1_s.at[s, 1], rs1_r.at[s, 1], to_y),
         )
 
     def rs2(q):
         s = q % SLOTS
         return (
-            remote(part.at[s, oy, x, 0], r2.at[s, 0], rs2_s.at[s, 0], rs2_r.at[s, 0], to_y),
-            remote(part.at[s, y, ox, 1], r2.at[s, 1], rs2_s.at[s, 1], rs2_r.at[s, 1], to_x),
+            remote(p2.at[s, 0], r2.at[s, 0], rs2_s.at[s, 0], rs2_r.at[s, 0], to_y),
+            remote(p2.at[s, 1], r2.at[s, 1], rs2_s.at[s, 1], rs2_r.at[s, 1], to_x),
         )
 
     def ag1(q):
@@ -238,7 +271,7 @@
 
     def gx_out(g):
         t = (g % tiles) // per_chunk
-        return pltpu.make_async_copy(gout.at[g % 2], gx_hbm.at[t, :, lanes(g)], go_sem.at[g % 2])
+        return pltpu.make_async_copy(gout.at[g % 2], gx_hbm.at[t, lanes(g)], go_sem.at[g % 2])
 
     def in_plane(n):
         there = (to_x, to_y, to_core)[n]
@@ -343,14 +376,17 @@
             for a in range(2):
                 for b in range(2):
                     part[s, a, b, t] = out[a, b]
+        for a in range(2):
+            p1[s, 0, a] = pack(part[s, a, ox, 0])
+            p1[s, 1, a] = pack(part[s, oy, a, 1])
 
     def reduce(q):
         s = q % SLOTS
         wait_recv(rs1(q))
-        part[s, oy, x, 0] = part[s, oy, x, 0] + r1[s, 0, oy]
-        part[s, y, ox, 1] = part[s, y, ox, 1] + r1[s, 1, ox]
-        part[s, y, x, 0] = part[s, y, x, 0] + r1[s, 0, y]
-        part[s, y, x, 1] = part[s, y, x, 1] + r1[s, 1, x]
+        p2[s, 0] = pack(part[s, oy, x, 0] + unpack(r1[s, 0, oy]))
+        p2[s, 1] = pack(part[s, y, ox, 1] + unpack(r1[s, 1, ox]))
+        part[s, y, x, 0] = part[s, y, x, 0] + unpack(r1[s, 0, y])
+        part[s, y, x, 1] = part[s, y, x, 1] + unpack(r1[s, 1, x])
 
     def pointwise(q):
         k, i, s = q // per_chunk, q % per_chunk, q % SLOTS
@@ -365,7 +401,7 @@
         mix = mix_ref[k]
         bias = [mix[:, t : t + 1] for t in range(2)]
         stitch = [[mix[:, 2 + 2 * a + b : 3 + 2 * a + b] for b in range(2)] for a in range(2)]
-        pre = [part[s, y, x, t] + r2[s, t] + bias[t] for t in range(2)]
+        pre = [part[s, y, x, t] + unpack(r2[s, t]) + bias[t] for t in range(2)]
         act = [jnp.maximum(p, 0.0) for p in pre]
         up = [cbuf[s, t].astype(F32) * valid for t in range(2)]
         cut = lanes(q)
@@ -527,8 +563,8 @@
             def _():
                 gx_out(g - 2).wait()
 
-            keep = 1.0 - pad_col_ref[...] * small_ref[g % per_chunk]
-            gout[g % 2] = (acc[g % 2] * keep).astype(BF16)
+            keep = (1.0 - image_ref[lanes(g), 0:1] * pad_row_ref[...]).astype(BF16)
+            gout[g % 2] = jnp.transpose(acc[g % 2].astype(BF16)) * keep
             gx_out(g).start()
 
     def sums(n):
@@ -577,8 +613,8 @@
     first = per_chunk + 3
 
     def body(s, carry):
-        stage(s, forward, rs1, rs1, rs2)
-        stage(s - 1, reduce, rs2)
+        stage(s, forward, rs1, rs1)
+        stage(s - 1, reduce, rs2, rs2)
         stage(s - 2, pointwise, ag1, ag1)
         stage(s - 3, spread, ag2, ag2)
         stage(s - 4, across, cx, cx)
@@ -684,21 +720,23 @@
         functools.partial(kernel, planes),
         out_shape=(
             jax.ShapeDtypeStruct((2, chunks, STEP, images), BF16),
-            jax.ShapeDtypeStruct((towers, width, images), BF16),
+            jax.ShapeDtypeStruct((towers, images, width), BF16),
             jax.ShapeDtypeStruct((2, halves, chunks, STEP, width), F32),
             jax.ShapeDtypeStruct((8, many), F32),
             jax.ShapeDtypeStruct((2, 2, 2, 2, chunks, STEP, images), BF16),
             jax.ShapeDtypeStruct((tiles, width, IMAGES), F32),
         ),
-        in_specs=[hbm] * 3 + [vmem] * 6,
+        in_specs=[hbm] * 3 + [vmem] * 4,
         out_specs=(hbm, hbm, hbm, vmem, hbm, hbm),
         scratch_shapes=[
             pltpu.VMEM((2, towers, images, width), BF16),
             pltpu.VMEM((2, towers, 4, width, 2 * STEP), BF16),
             pltpu.VMEM((2, towers, 2, 4, STEP, width), BF16),
             pltpu.VMEM((SLOTS, 2, 2, towers, STEP, IMAGES), F32),
-            pltpu.VMEM((SLOTS, 2, 2, STEP, IMAGES), F32),
-            pltpu.VMEM((SLOTS, 2, STEP, IMAGES), F32),
+            pltpu.VMEM((SLOTS, 2, 2, WORDS, IMAGES), jnp.int32),
+            pltpu.VMEM((SLOTS, 2, WORDS, IMAGES), jnp.int32),
+            pltpu.VMEM((SLOTS, 2, 2, WORDS, IMAGES), jnp.int32),
+            pltpu.VMEM((SLOTS, 2, WORDS, IMAGES), jnp.int32),
             pltpu.VMEM((2, towers, 2, 2, 2, STEP, images), BF16),
             pltpu.VMEM((SLOTS, 2, STEP, IMAGES), BF16),
             pltpu.VMEM((SLOTS, 2, STEP, IMAGES), BF16),
@@ -713,7 +751,7 @@
             pltpu.VMEM((width, 16 * STEP), BF16),
             pltpu.VMEM((2, 2, 2, 2, 2, STEP, IMAGES), BF16),
             pltpu.VMEM((2, width, IMAGES), F32),
-            pltpu.VMEM((2, width, IMAGES), BF16),
+            pltpu.VMEM((2, IMAGES, width), BF16),
             pltpu.VMEM((3, 8, 128), F32),
             pltpu.VMEM((3, 8, 128), F32),
             pltpu.VMEM((planes, 8, many), F32),
@@ -760,16 +798,14 @@
         cotangent.reshape(2, chunks, STEP, images),
         jnp.stack([small, weight_valid], axis=1),
         padded[None, :],
-        padded[:, None],
         weight_valid.reshape(per_chunk, 1, IMAGES),
-        small.reshape(per_chunk, 1, IMAGES),
         jnp.transpose(mix, (1, 2, 0)),
     )
     grad_weights = jnp.transpose(grad_weights.reshape(towers, -1, width), (0, 2, 1))
     grads = jnp.transpose(stats[0, :-128].reshape(chunks, 6, STEP), (1, 0, 2)).reshape(6, mine)
     return (
         stitched.reshape(2, mine, images),
-        jnp.transpose(grad_inputs, (0, 2, 1)),
+        grad_inputs,
         grad_weights,
         grads[:2],
         grads[2:].reshape(2, 2, mine),

time: 544 us -> 453 us (0.83)
  Pallas kernels: 498 us -> 413 us
    pallas_call x1, Pallas kernels: 498 us -> 413 us  [fused(): pl.pallas_call(functools.partial(kernel, planes), out_shape=(jax.ShapeDty...]
    unnamed x6 -> x4, local copies, waits for them, and re-layouts: 17.4 us -> 12.9 us
where the time goes in v4:
time: 453 us; the launch traced here: 450 us
  Pallas kernels  413 us (91%)
  local copies, waits for them, and re-layouts  29.2 us (6%)
    pallas_call x1, Pallas kernels, fused(): pl.pallas_call(functools.partial(kernel, planes), out_shape=(jax.ShapeDty...  413 us
    unnamed x4, local copies, waits for them, and re-layouts  12.9 us
    reshape x1, local copies, waits for them, and re-layouts, fused(): grad_weights.reshape(towers, -1, width)  9.58 us

profile of v4, /device:TPU:8, one launch (start us, length us, event | category | flops | bytes accessed | tf_op | source)
XLA Modules:
  0.0 449.7 jit_solution(14505402458182183421)
XLA Ops:
  0.6 0.7 or_convert_fusion.pad_row_ref
  1.3 0.7 convert_element_type.14
  2.0 0.0 copy-start
  2.0 0.8 concatenate.8
  2.8 0.7 compare_convert_fusion
  3.5 0.0 copy-done
  3.5 0.8 concatenate.9
  4.3 0.9 copy.30
  5.1 1.3 copy.31.image_ref
  6.5 413.1 %towers.1 = (bf16[2,8,64,2048]{3,2,1,0:T(8,128)(2,1)}, bf16[2,2048,1152]{2,1,0:T(8,128)(2,1)}, f32[2,2,8,64,1152]{4,3,2,1,0:T(8,128)}, f32[8,3200]{1,0:T(8,128)}...) custom-call(bf16[2,2048,1152]{2,1,0:T(8,128)(2,1)} %x_hbm.1, bf16[2,1152,4096]{2,1,0:T(8,128)(2,1)} %w_hbm.1, ...), custom_call_target="tpu_custom_call" | custom-call | tf_op jit(solution)/shard_map/towers/pallas_call | solution.py:719
  419.6 0.8 slice_reduce_fusion.1
  420.4 0.9 slice_reduce_fusion
  421.3 0.6 fusion
  425.2 0.6 maximum_sqrt_fusion
  425.8 0.1 reshape_squeeze.3
  425.9 0.7 reshape.120
  426.5 0.7 slice.30
  427.2 9.6 %copy.32 = f32[2,1024,1152]{1,2,0:T(8,128)} copy(f32[2,1024,1152]{2,1,0:T(8,128)} %bitcast.9) | data formatting | bytes 18874368 | tf_op jit(solution)/shard_map/reshape | solution.py:804
  436.8 4.8 %copy.37 = bf16[2,512,2048]{2,1,0:T(8,128)(2,1)} copy(bf16[2,512,2048]{2,1,0:T(8,128)(2,1)} %bitcast.11) | data formatting | bytes 8388608
  441.6 8.1 %copy.38 = bf16[2,2048,1152]{2,1,0:T(8,128)(2,1)} copy(bf16[2,2048,1152]{2,1,0:T(8,128)(2,1)} %get-tuple-element.25) | data formatting | bytes 18874368
  (6 shorter events, 0.0 us)
Async XLA Ops:
  2.0 1.5 copy-start

commit v5 on v4

--- a/solution.py
+++ b/solution.py
@@ -2,6 +2,7 @@
 
 import jax
 import jax.numpy as jnp
+import numpy as np
 from jax import lax
 from jax.experimental import pallas as pl
 from jax.experimental.pallas import tpu as pltpu
@@ -67,16 +68,22 @@
     x_hbm,
     w_hbm,
     cot_hbm,
-    image_ref,
+    valid_in,
+    class_in,
     pad_row_ref,
-    valid_ref,
-    mix_ref,
+    bias_in,
+    stitch_in,
     st_hbm,
     gx_hbm,
     gw_hbm,
-    stats_ref,
+    bias_out,
+    stitch_out,
+    rms_out,
     g_hbm,
     acc_hbm,
+    image_ref,
+    valid_ref,
+    mix_ref,
     xb,
     raw,
     wt,
@@ -352,7 +359,7 @@
             x_local(i).wait()
             x_remote(i).wait_recv()
             keep = (1.0 - image_ref[cut, 0:1] * pad_row_ref[...]).astype(BF16)
-            valid = image_ref[cut, 1:2]
+            valid = image_ref[cut, 64:65]
             for t in range(towers):
                 used = xb[0, t, cut] * keep
                 xb[0, t, cut] = used
@@ -426,17 +433,17 @@
         wait_recv(ag2(q))
 
     def terms(k, n):
-        third = width // 3
-        for t in range(towers):
+        unit = width // 3
+        for t, at, wide in (((0, 0, 2 * unit),), ((0, 2 * unit, unit), (1, 0, unit)), ((1, unit, 2 * unit),))[n]:
             value = jnp.dot(
                 gfull[k % 2, t].reshape(8 * STEP, images),
-                xb[0, t, :, n * third : (n + 1) * third],
+                xb[0, t, :, at : at + wide],
                 preferred_element_type=F32,
             )
-            value = value.astype(BF16).reshape(planes, halves, STEP, third)
+            value = value.astype(BF16).reshape(planes, halves, STEP, wide)
             for d in range(planes):
                 for e in range(halves):
-                    zo[t, d, e, :, n * third : (n + 1) * third] = value[d, e]
+                    zo[t, d, e, :, at : at + wide] = value[d, e]
 
     def chain(k, j):
         if j == planes - 2:
@@ -594,6 +601,19 @@
     start(w_local(0))
     for i in range(per_chunk):
         x_local(i).start()
+    for i in range(per_chunk):
+        cut = slice(i * IMAGES, (i + 1) * IMAGES)
+        valid = valid_in[:, cut].astype(F32)
+        small = jnp.where(class_in[:, cut] == 195, 1.0, 0.0)
+        valid_ref[i] = valid
+        both = jnp.concatenate(
+            [jnp.broadcast_to(small, (64, IMAGES)), jnp.broadcast_to(valid, (64, IMAGES))], axis=0
+        )
+        image_ref[cut] = jnp.transpose(both)
+    mix = jnp.concatenate(
+        [bias_in[...], stitch_in[0], stitch_in[1], jnp.zeros((122, mine), F32)], axis=0
+    )
+    mix_ref[...] = jnp.transpose(mix).reshape(chunks, STEP, 128)
     pl.semaphore_wait(barrier, 2 + planes)
     start(w_remote(0))
 
@@ -696,7 +716,46 @@
     for off in range(1, planes):
         to_plane(off).wait_send()
         from_plane(off).wait_recv()
-    stats_ref[...] = sum(stats[d] for d in range(planes))
+    every = sum(stats[d] for d in range(planes))
+    for k in range(chunks):
+        for n in range(6):
+            at = (k * 6 + n) * STEP
+            value = every[0:1, at : at + STEP]
+            if n < 2:
+                bias_out[n : n + 1, k * STEP : (k + 1) * STEP] = value
+            else:
+                stitch_out[(n - 2) // 2, n % 2 : n % 2 + 1, k * STEP : (k + 1) * STEP] = value
+    ends = jnp.sum(every[:, chunks * 6 * STEP :], axis=1, keepdims=True)
+    images_in = ends[3:4] / lax.axis_size("rows")
+    for n, size in enumerate((F, C, C)):
+        rms_out[n : n + 1] = jnp.broadcast_to(jnp.sqrt(ends[n : n + 1] / (images_in * 2 * size)), (1, 128))
+
+
+def put_out(st_ref, gx_ref, gw_ref, st_out, gx_out, gw_out):
+    st_out[...] = st_ref[...]
+    gx_out[...] = gx_ref[...]
+    gw_out[0] = jnp.transpose(gw_ref[0])
+
+
+def results(stitched, grad_inputs, grad_weights):
+    towers, width = grad_weights.shape[0], grad_weights.shape[2]
+    mine = grad_weights.shape[1]
+    each = mine // 128
+    steps = towers * each
+    flat = [v.reshape(-1, v.shape[-1]) for v in (stitched, grad_inputs)]
+    plain = [pl.BlockSpec((v.shape[0] // steps, v.shape[1]), lambda i: (i, 0)) for v in flat]
+    out = pl.pallas_call(
+        put_out,
+        grid=(steps,),
+        out_shape=(
+            *(jax.ShapeDtypeStruct(v.shape, v.dtype) for v in flat),
+            jax.ShapeDtypeStruct((towers, width, mine), F32),
+        ),
+        in_specs=[*plain, pl.BlockSpec((1, 128, width), lambda i: (i // each, i % each, 0))],
+        out_specs=[*plain, pl.BlockSpec((1, width, 128), lambda i: (i // each, 0, i % each))],
+        name="results",
+    )(*flat, grad_weights)
+    return out[0].reshape(stitched.shape), out[1].reshape(grad_inputs.shape), out[2]
 
 
 def fused(inputs, weights, bias, stitch, cotangent, valid, size_class):
@@ -707,28 +766,30 @@
     per_chunk = images // IMAGES
     halves = 8 // planes
     tiles = towers * per_chunk
-    small = (size_class == 195).astype(F32)
-    place = lax.iota(jnp.int32, width) % 36
-    padded = ((place // 6 == 5) | (place % 6 == 5)).astype(F32)
-    weight_valid = valid.astype(F32)
-    mix = jnp.concatenate([bias, stitch.reshape(4, mine)], axis=0).reshape(6, chunks, STEP)
+    place = np.arange(width) % 36
+    padded = ((place // 6 == 5) | (place % 6 == 5)).astype(np.float32)
     many = chunks * 6 * STEP + 128
     vmem = pl.BlockSpec(memory_space=pltpu.VMEM)
     hbm = pl.BlockSpec(memory_space=pl.ANY)
     dma = pltpu.SemaphoreType.DMA
-    stitched, grad_inputs, grad_weights, stats, _, _ = pl.pallas_call(
+    stitched, grad_inputs, grad_weights, grad_bias, grad_stitch, means, _, _ = pl.pallas_call(
         functools.partial(kernel, planes),
         out_shape=(
             jax.ShapeDtypeStruct((2, chunks, STEP, images), BF16),
             jax.ShapeDtypeStruct((towers, images, width), BF16),
             jax.ShapeDtypeStruct((2, halves, chunks, STEP, width), F32),
-            jax.ShapeDtypeStruct((8, many), F32),
+            jax.ShapeDtypeStruct((2, mine), F32),
+            jax.ShapeDtypeStruct((2, 2, mine), F32),
+            jax.ShapeDtypeStruct((8, 128), F32),
             jax.ShapeDtypeStruct((2, 2, 2, 2, chunks, STEP, images), BF16),
             jax.ShapeDtypeStruct((tiles, width, IMAGES), F32),
         ),
-        in_specs=[hbm] * 3 + [vmem] * 4,
-        out_specs=(hbm, hbm, hbm, vmem, hbm, hbm),
+        in_specs=[hbm] * 3 + [vmem] * 5,
+        out_specs=(hbm, hbm, hbm, vmem, vmem, vmem, hbm, hbm),
         scratch_shapes=[
+            pltpu.VMEM((images, 128), F32),
+            pltpu.VMEM((per_chunk, 1, IMAGES), F32),
+            pltpu.VMEM((chunks, STEP, 128), F32),
             pltpu.VMEM((2, towers, images, width), BF16),
             pltpu.VMEM((2, towers, 4, width, 2 * STEP), BF16),
             pltpu.VMEM((2, towers, 2, 4, STEP, width), BF16),
@@ -796,21 +857,16 @@
         inputs,
         weights,
         cotangent.reshape(2, chunks, STEP, images),
-        jnp.stack([small, weight_valid], axis=1),
+        valid[None, :],
+        size_class[None, :],
         padded[None, :],
-        weight_valid.reshape(per_chunk, 1, IMAGES),
-        jnp.transpose(mix, (1, 2, 0)),
+        bias,
+        stitch,
     )
-    grad_weights = jnp.transpose(grad_weights.reshape(towers, -1, width), (0, 2, 1))
-    grads = jnp.transpose(stats[0, :-128].reshape(chunks, 6, STEP), (1, 0, 2)).reshape(6, mine)
-    return (
-        stitched.reshape(2, mine, images),
-        grad_inputs,
-        grad_weights,
-        grads[:2],
-        grads[2:].reshape(2, 2, mine),
-        rms(jnp.sum(stats[:4, -128:], axis=1)),
+    stitched, grad_inputs, grad_weights = results(
+        stitched.reshape(2, mine, images), grad_inputs, grad_weights.reshape(towers, -1, width)
     )
+    return (stitched, grad_inputs, grad_weights, grad_bias, grad_stitch, means[:3, 0])
 
 
 def rms(totals):

time: 453 us -> 432 us (0.954)
  local copies, waits for them, and re-layouts: 29.2 us -> 1.83 us
  Pallas kernels: 413 us -> 427 us
    pallas_call x0 -> x1, Pallas kernels: none -> 21.3 us  [results(): pl.pallas_call(put_out, grid=(steps,), out_shape=(*(jax.ShapeDtypeStruct(...]
    unnamed x4 -> x8, local copies, waits for them, and re-layouts: 12.9 us -> 1.2 us
    reshape x2 -> x0, local copies, waits for them, and re-layouts: 10.3 us -> none  [the longest x1 9.58 us: fused(): grad_weights.reshape(towers, -1, width)]
    pallas_call x1, Pallas kernels: 413 us -> 406 us  [fused(): pl.pallas_call(functools.partial(kernel, planes), out_shape=(jax.ShapeDty...]
where the time goes in v5:
time: 432 us; the launch traced here: 429 us
  Pallas kernels  427 us (99%)
    pallas_call x1, Pallas kernels, fused(): pl.pallas_call(functools.partial(kernel, planes), out_shape=(jax.ShapeDty...  406 us
    pallas_call x1, Pallas kernels, results(): pl.pallas_call(put_out, grid=(steps,), out_shape=(*(jax.ShapeDtypeStruct(...  21.3 us

profile of v5, /device:TPU:8, one launch (start us, length us, event | category | flops | bytes accessed | tf_op | source)
XLA Modules:
  0.0 429.4 jit_solution(17604606281715951603)
XLA Ops:
  0.6 405.6 %towers.1 = (bf16[2,8,64,2048]{3,2,1,0:T(8,128)(2,1)}, bf16[2,2048,1152]{2,1,0:T(8,128)(2,1)}, f32[2,2,8,64,1152]{4,3,2,1,0:T(8,128)}, f32[2,512]{1,0:T(2,128)},...) custom-call(bf16[2,2048,1152]{2,1,0:T(8,128)(2,1)} %x_hbm.1, ...), custom_call_target="tpu_custom_call" | custom-call | tf_op jit(solution)/shard_map/towers/pallas_call | solution.py:775
  406.2 0.0 copy-start.2
  406.2 0.0 copy-start.1
  406.2 0.0 copy-start
  406.3 21.3 %results.1 = (bf16[1024,2048]{1,0:T(8,128)(2,1)}, bf16[4096,1152]{1,0:T(8,128)(2,1)}, f32[2,1152,1024]{2,1,0:T(8,128)}) custom-call(bf16[1024,2048]{1,0:T(8,128)(2,1)} %bitcast.11, bf16[4096,1152]{1,0:T(8,128)(2,1)} %bitcast.8, f32[2,1024,1152]{2,1,0:T(8,128)} %bitcast.9), custom_call_target="tpu_custom_call" | custom-call | tf_op jit(solution)/shard_map/results/pallas_call | solution.py:747
  427.6 0.0 copy-done.2
  427.6 0.6 slice_reduce_fusion
  428.2 0.0 copy-done.1
  428.2 0.6 copy.16
  428.8 0.0 copy-done
  428.8 0.6 copy.17
Async XLA Ops:
  406.2 21.4 %copy-start.2 = (f32[8,128]{1,0:T(8,128)S(1)}, f32[8,128]{1,0:T(8,128)}, u32[]{:S(2)}) copy-start(f32[8,128]{1,0:T(8,128)} %get-tuple-element.23) | copy-start | bytes 12292
  406.2 22.0 %copy-start.1 = (f32[2,512]{1,0:T(2,128)S(1)}, f32[2,512]{1,0:T(2,128)}, u32[]{:S(2)}) copy-start(f32[2,512]{1,0:T(2,128)} %get-tuple-element.33) | copy-start | bytes 12292
  406.2 22.6 %copy-start = (f32[2,2,512]{2,1,0:T(2,128)S(1)}, f32[2,2,512]{2,1,0:T(2,128)}, u32[]{:S(2)}) copy-start(f32[2,2,512]{2,1,0:T(2,128)} %get-tuple-element.34) | copy-start | bytes 24580

commit v6 on v5

--- a/solution.py
+++ b/solution.py
@@ -14,6 +14,8 @@
 STEP = 64
 IMAGES = 256
 SLOTS = 4
+HELD = 3
+EACH = 6
 WORDS = 40
 TOP = 2.0**18 - 2.0
 F32 = jnp.float32
@@ -267,14 +269,14 @@
     def g_load(g):
         p, t, i = g // tiles, (g % tiles) // per_chunk, g % per_chunk
         return pltpu.make_async_copy(
-            g_hbm.at[t, :, :, :, pl.ds(p * 2, 2), :, lanes(i)], gtile.at[g % 2], gt_sem.at[g % 2]
+            g_hbm.at[t, :, :, :, pl.ds(p * 2, 2), :, lanes(i)], gtile.at[g % HELD], gt_sem.at[g % HELD]
         )
 
     def acc_in(g):
-        return pltpu.make_async_copy(acc_hbm.at[g % tiles], acc.at[g % 2], ai_sem.at[g % 2])
+        return pltpu.make_async_copy(acc_hbm.at[g % tiles], acc.at[g % HELD], ai_sem.at[g % HELD])
 
     def acc_out(g):
-        return pltpu.make_async_copy(acc.at[g % 2], acc_hbm.at[g % tiles], ao_sem.at[g % 2])
+        return pltpu.make_async_copy(acc.at[g % HELD], acc_hbm.at[g % tiles], ao_sem.at[g % HELD])
 
     def gx_out(g):
         t = (g % tiles) // per_chunk
@@ -319,7 +321,6 @@
     def turn(p):
         for c in w_local(p):
             c.wait()
-        wait_recv(w_remote(p))
 
         def one(n, carry):
             side, t, c = n // 8, (n // 4) % 2, n % 4
@@ -328,7 +329,9 @@
             wt[side, t, 1, c] = turned[STEP:]
             return carry
 
-        lax.fori_loop(0, 16, one, 0)
+        lax.fori_loop(0, 8, one, 0)
+        wait_recv(w_remote(p))
+        lax.fori_loop(8, 16, one, 0)
 
         @pl.when(p + 1 < pairs)
         def _():
@@ -527,13 +530,9 @@
     def prepare(g):
         g_load(g).start()
 
-        @pl.when(g % per_chunk == 0)
-        def _():
-            start(wg_load(g))
-
-        @pl.when((g >= 2) & (g - 2 < (pairs - 1) * tiles))
-        def _():
-            acc_out(g - 2).wait()
+        @pl.when((g >= HELD) & (g - HELD < (pairs - 1) * tiles))
+        def _():
+            acc_out(g - HELD).wait()
 
         @pl.when(g >= tiles)
         def _():
@@ -548,31 +547,40 @@
                 c.wait()
 
         value = jnp.dot(
-            wgx[...], gtile[g % 2].reshape(16 * STEP, IMAGES), preferred_element_type=F32
+            wgx[...], gtile[g % HELD].reshape(16 * STEP, IMAGES), preferred_element_type=F32
         )
+        final = g >= (pairs - 1) * tiles
 
         @pl.when(g < tiles)
         def _():
-            acc[g % 2] = value
+            acc[g % HELD] = value
 
         @pl.when(g >= tiles)
         def _():
             acc_in(g).wait()
-            acc[g % 2] = acc[g % 2] + value
-
-        @pl.when(g < (pairs - 1) * tiles)
+            acc[g % HELD] = acc[g % HELD] + value
+
+        @pl.when(jnp.logical_not(final))
         def _():
             acc_out(g).start()
 
-        @pl.when(g >= (pairs - 1) * tiles)
+        @pl.when(final)
         def _():
             @pl.when(g >= (pairs - 1) * tiles + 2)
             def _():
                 gx_out(g - 2).wait()
 
             keep = (1.0 - image_ref[lanes(g), 0:1] * pad_row_ref[...]).astype(BF16)
-            gout[g % 2] = jnp.transpose(acc[g % 2].astype(BF16)) * keep
+            gout[g % 2] = jnp.transpose(acc[g % HELD].astype(BF16)) * keep
             gx_out(g).start()
+
+        @pl.when(((g + 1) % per_chunk == 0) & (g + 1 < pairs * tiles))
+        def _():
+            start(wg_load(g + 1))
+
+        @pl.when(g + 2 < pairs * tiles)
+        def _():
+            prepare(g + 2)
 
     def sums(n):
         if n == 0:
@@ -629,8 +637,9 @@
 
     ready = per_chunk - 1 + 5
     offsets = [2 + 3 * j for j in range(planes)]
-    ends = [2 + 5 * j for j in range(planes)]
+    ends = [2 + 10 * j for j in range(planes)]
     first = per_chunk + 3
+    late = (chunks - 1) * per_chunk + 3
 
     def body(s, carry):
         stage(s, forward, rs1, rs1)
@@ -677,19 +686,32 @@
                         g_copy(k).wait()
 
             step(0)
-            g = done - first
-
-            @pl.when((g >= 0) & (g < pairs * tiles))
+            @pl.when(done == first - 1)
+            def _():
+                start(wg_load(0))
+                prepare(0)
+                prepare(1)
+
+            since = done - first
+            usual = (since >= 0) & (since % per_chunk < 5) & (since // per_chunk < chunks - 2)
+            g = jnp.where(
+                done >= late,
+                done - late + EACH * (chunks - 2),
+                EACH * (since // per_chunk) + since % per_chunk,
+            )
+
+            @pl.when(usual | ((done >= late) & (g < pairs * tiles)))
             def _():
                 tile(g)
 
-            @pl.when((g >= -1) & (g < pairs * tiles - 1))
+            @pl.when(usual & (since % per_chunk == 4))
             def _():
-                prepare(g + 1)
+                tile(g + 1)
 
         return carry
 
-    lax.fori_loop(0, ready + max((chunks - 1) * per_chunk + ends[-1], first + pairs * tiles - 1) + 1, body, 0)
+    left = pairs * tiles - EACH * (chunks - 2)
+    lax.fori_loop(0, ready + max((chunks - 1) * per_chunk + ends[-1], late + left - 1) + 1, body, 0)
 
     def drain(q, carry):
         st_copy(q).wait()
@@ -740,7 +762,8 @@
 def results(stitched, grad_inputs, grad_weights):
     towers, width = grad_weights.shape[0], grad_weights.shape[2]
     mine = grad_weights.shape[1]
-    each = mine // 128
+    block = min(mine, 512)
+    each = mine // block
     steps = towers * each
     flat = [v.reshape(-1, v.shape[-1]) for v in (stitched, grad_inputs)]
     plain = [pl.BlockSpec((v.shape[0] // steps, v.shape[1]), lambda i: (i, 0)) for v in flat]
@@ -751,8 +774,8 @@
             *(jax.ShapeDtypeStruct(v.shape, v.dtype) for v in flat),
             jax.ShapeDtypeStruct((towers, width, mine), F32),
         ),
-        in_specs=[*plain, pl.BlockSpec((1, 128, width), lambda i: (i // each, i % each, 0))],
-        out_specs=[*plain, pl.BlockSpec((1, width, 128), lambda i: (i // each, 0, i % each))],
+        in_specs=[*plain, pl.BlockSpec((1, block, width), lambda i: (i // each, i % each, 0))],
+        out_specs=[*plain, pl.BlockSpec((1, width, block), lambda i: (i // each, 0, i % each))],
         name="results",
     )(*flat, grad_weights)
     return out[0].reshape(stitched.shape), out[1].reshape(grad_inputs.shape), out[2]
@@ -810,8 +833,8 @@
             pltpu.VMEM((2, STEP, 128), F32),
             pltpu.VMEM((1, width), F32),
             pltpu.VMEM((width, 16 * STEP), BF16),
-            pltpu.VMEM((2, 2, 2, 2, 2, STEP, IMAGES), BF16),
-            pltpu.VMEM((2, width, IMAGES), F32),
+            pltpu.VMEM((HELD, 2, 2, 2, 2, STEP, IMAGES), BF16),
+            pltpu.VMEM((HELD, width, IMAGES), F32),
             pltpu.VMEM((2, IMAGES, width), BF16),
             pltpu.VMEM((3, 8, 128), F32),
             pltpu.VMEM((3, 8, 128), F32),
@@ -840,9 +863,9 @@
             dma,
             pltpu.SemaphoreType.REGULAR((2, planes - 1)),
             dma((8,)),
-            dma((2,)),
-            dma((2,)),
-            dma((2,)),
+            dma((HELD,)),
+            dma((HELD,)),
+            dma((HELD,)),
             dma((2,)),
             dma((3,)),
             dma((3,)),

time: 432 us -> 423 us (0.979)
  Pallas kernels: 427 us -> 421 us
    pallas_call x1, Pallas kernels: 21.3 us -> 15.3 us  [results(): pl.pallas_call(put_out, grid=(steps,), out_shape=(*(jax.ShapeDtypeStruct(...]
where the time goes in v6:
time: 423 us
  Pallas kernels  421 us (100%)
    pallas_call x1, Pallas kernels, fused(): pl.pallas_call(functools.partial(kernel, planes), out_shape=(jax.ShapeDty...  405 us
    pallas_call x1, Pallas kernels, results(): pl.pallas_call(put_out, grid=(steps,), out_shape=(*(jax.ShapeDtypeStruct(...  15.3 us

profile of v6, /device:TPU:8, one launch (start us, length us, event | category | flops | bytes accessed | tf_op | source)
XLA Modules:
  0.0 423.1 jit_solution(5141625268227077469)
XLA Ops:
  0.6 405.2 %towers.1 = (bf16[2,8,64,2048]{3,2,1,0:T(8,128)(2,1)}, bf16[2,2048,1152]{2,1,0:T(8,128)(2,1)}, f32[2,2,8,64,1152]{4,3,2,1,0:T(8,128)}, f32[2,512]{1,0:T(2,128)},...) custom-call(bf16[2,2048,1152]{2,1,0:T(8,128)(2,1)} %x_hbm.1, ...), custom_call_target="tpu_custom_call" | custom-call | tf_op jit(solution)/shard_map/towers/pallas_call | solution.py:798
  405.8 0.0 copy-start.2
  405.9 0.0 copy-start.1
  405.9 0.0 copy-start
  405.9 15.3 %results.1 = (bf16[1024,2048]{1,0:T(8,128)(2,1)}, bf16[4096,1152]{1,0:T(8,128)(2,1)}, f32[2,1152,1024]{2,1,0:T(8,128)}) custom-call(bf16[1024,2048]{1,0:T(8,128)(2,1)} %bitcast.11, bf16[4096,1152]{1,0:T(8,128)(2,1)} %bitcast.8, f32[2,1024,1152]{2,1,0:T(8,128)} %bitcast.9), custom_call_target="tpu_custom_call" | custom-call | tf_op jit(solution)/shard_map/results/pallas_call | solution.py:770
  421.2 0.0 copy-done.2
  421.2 0.6 slice_reduce_fusion
  421.9 0.0 copy-done.1
  421.9 0.6 copy.16
  422.5 0.0 copy-done
  422.5 0.6 copy.17
Async XLA Ops:
  405.8 15.4 %copy-start.2 = (f32[8,128]{1,0:T(8,128)S(1)}, f32[8,128]{1,0:T(8,128)}, u32[]{:S(2)}) copy-start(f32[8,128]{1,0:T(8,128)} %get-tuple-element.23) | copy-start | bytes 12292
  405.9 16.0 %copy-start.1 = (f32[2,512]{1,0:T(2,128)S(1)}, f32[2,512]{1,0:T(2,128)}, u32[]{:S(2)}) copy-start(f32[2,512]{1,0:T(2,128)} %get-tuple-element.33) | copy-start | bytes 12292
  405.9 16.6 %copy-start = (f32[2,2,512]{2,1,0:T(2,128)S(1)}, f32[2,2,512]{2,1,0:T(2,128)}, u32[]{:S(2)}) copy-start(f32[2,2,512]{2,1,0:T(2,128)} %get-tuple-element.34) | copy-start | bytes 24580

commit v7 on v6

--- a/solution.py
+++ b/solution.py
@@ -319,19 +319,20 @@
             start(sends(q))
 
     def turn(p):
-        for c in w_local(p):
-            c.wait()
-
-        def one(n, carry):
-            side, t, c = n // 8, (n // 4) % 2, n % 4
-            turned = jnp.transpose(raw[side, t, c])
-            wt[side, t, 0, c] = turned[:STEP]
-            wt[side, t, 1, c] = turned[STEP:]
-            return carry
-
-        lax.fori_loop(0, 8, one, 0)
-        wait_recv(w_remote(p))
-        lax.fori_loop(8, 16, one, 0)
+        for side, copies in enumerate((w_local(p), w_remote(p))):
+            for c, copy in enumerate(copies):
+                if side == 0:
+                    copy.wait()
+                else:
+                    copy.wait_recv()
+
+                def one(t, carry):
+                    turned = jnp.transpose(raw[side, t, c])
+                    wt[side, t, 0, c] = turned[:STEP]
+                    wt[side, t, 1, c] = turned[STEP:]
+                    return carry
+
+                lax.fori_loop(0, towers, one, 0)
 
         @pl.when(p + 1 < pairs)
         def _():
@@ -342,18 +343,6 @@
         p, h = k // 2, k % 2
 
         cot_copy(q).start()
-
-        @pl.when((i == 0) & (h == 0))
-        def _():
-            turn(p)
-
-        @pl.when((i == 0) & (h == 1))
-        def _():
-            wait_send(w_remote(p))
-
-            @pl.when(p + 1 < pairs)
-            def _():
-                start(w_remote(p + 1))
 
         cut = pl.ds(pl.multiple_of(i * IMAGES, IMAGES), IMAGES)
 
@@ -369,6 +358,18 @@
                 used = used.astype(F32)
                 usq_ref[...] = usq_ref[...] + jnp.sum(used * used * valid, axis=0, keepdims=True)
                 xb[1, t, cut] = xb[1, t, cut] * keep
+
+        @pl.when((i == 0) & (h == 0))
+        def _():
+            turn(p)
+
+        @pl.when((i == 0) & (h == 1))
+        def _():
+            wait_send(w_remote(p))
+
+            @pl.when(p + 1 < pairs)
+            def _():
+                start(w_remote(p + 1))
 
         for t in range(towers):
             out = lax.dot_general(
@@ -623,13 +624,14 @@
     )
     mix_ref[...] = jnp.transpose(mix).reshape(chunks, STEP, 128)
     pl.semaphore_wait(barrier, 2 + planes)
+    x_remote(0).start()
     start(w_remote(0))
 
     def send_x(i, carry):
         x_remote(i).start()
         return carry
 
-    lax.fori_loop(0, per_chunk, send_x, 0)
+    lax.fori_loop(1, per_chunk, send_x, 0)
     gb_ref[...] = jnp.zeros_like(gb_ref)
     gs_ref[...] = jnp.zeros_like(gs_ref)
     sq_ref[...] = jnp.zeros_like(sq_ref)

time: 423 us -> 423 us (level)
  no operation moved by 1% of the time
where the time goes in v7:
time: 423 us
  Pallas kernels  420 us (99%)
    pallas_call x1, Pallas kernels, fused(): pl.pallas_call(functools.partial(kernel, planes), out_shape=(jax.ShapeDty...  405 us
    pallas_call x1, Pallas kernels, results(): pl.pallas_call(put_out, grid=(steps,), out_shape=(*(jax.ShapeDtypeStruct(...  15.3 us

profile of v7, /device:TPU:8, one launch (start us, length us, event | category | flops | bytes accessed | tf_op | source)
XLA Modules:
  0.0 422.7 jit_solution(9354346070760446214)
XLA Ops:
  0.6 404.8 %towers.1 = (bf16[2,8,64,2048]{3,2,1,0:T(8,128)(2,1)}, bf16[2,2048,1152]{2,1,0:T(8,128)(2,1)}, f32[2,2,8,64,1152]{4,3,2,1,0:T(8,128)}, f32[2,512]{1,0:T(2,128)},...) custom-call(bf16[2,2048,1152]{2,1,0:T(8,128)(2,1)} %x_hbm.1, ...), custom_call_target="tpu_custom_call" | custom-call | tf_op jit(solution)/shard_map/towers/pallas_call | solution.py:800
  405.5 0.0 copy-start.2
  405.5 0.0 copy-start.1
  405.5 0.0 copy-start
  405.5 15.3 %results.1 = (bf16[1024,2048]{1,0:T(8,128)(2,1)}, bf16[4096,1152]{1,0:T(8,128)(2,1)}, f32[2,1152,1024]{2,1,0:T(8,128)}) custom-call(bf16[1024,2048]{1,0:T(8,128)(2,1)} %bitcast.11, bf16[4096,1152]{1,0:T(8,128)(2,1)} %bitcast.8, f32[2,1024,1152]{2,1,0:T(8,128)} %bitcast.9), custom_call_target="tpu_custom_call" | custom-call | tf_op jit(solution)/shard_map/results/pallas_call | solution.py:772
  420.8 0.0 copy-done.2
  420.8 0.6 slice_reduce_fusion
  421.5 0.0 copy-done.1
  421.5 0.6 copy.16
  422.1 0.0 copy-done
  422.1 0.6 copy.17
Async XLA Ops:
  405.5 15.4 %copy-start.2 = (f32[8,128]{1,0:T(8,128)S(1)}, f32[8,128]{1,0:T(8,128)}, u32[]{:S(2)}) copy-start(f32[8,128]{1,0:T(8,128)} %get-tuple-element.23) | copy-start | bytes 12292
  405.5 16.0 %copy-start.1 = (f32[2,512]{1,0:T(2,128)S(1)}, f32[2,512]{1,0:T(2,128)}, u32[]{:S(2)}) copy-start(f32[2,512]{1,0:T(2,128)} %get-tuple-element.33) | copy-start | bytes 12292
  405.5 16.6 %copy-start = (f32[2,2,512]{2,1,0:T(2,128)S(1)}, f32[2,2,512]{2,1,0:T(2,128)}, u32[]{:S(2)}) copy-start(f32[2,2,512]{2,1,0:T(2,128)} %get-tuple-element.34) | copy-start | bytes 24580

commit v8 on v7

--- a/solution.py
+++ b/solution.py
@@ -473,45 +473,50 @@
                         z_free.at[way, j - 1], inc=1, device_id=source, device_id_type=MESH
                     )
 
-            if j <= planes - 2:
-
-                @pl.when(near <= j)
+            def put(n, fill):
+                @pl.when(k > 0)
                 def _():
-                    dest = last - j + z if way == 0 else j - last + z
-
-                    @pl.when(k > 0)
-                    def _():
-                        z_copy(k - 1, j, way).wait_send()
-
-                    if j > 0:
-
-                        @pl.when(near >= 1)
-                        def _():
-                            z_copy(k, j - 1, way).wait_recv()
-
-                            def add(i, carry):
-                                t, e = i // halves, i % halves
-                                value = zo[t, dest, e].astype(F32) + zrecv[way, j - 1, t, e].astype(F32)
-                                zsend[way, j, t, e] = value.astype(BF16)
-                                return carry
-
-                            lax.fori_loop(0, towers * halves, add, 0)
-                            freed()
-
-                        @pl.when(near == 0)
-                        def _():
-                            zsend[way, j] = zo[:, dest]
-
-                    else:
-                        zsend[way, j] = zo[:, dest]
-
-                    @pl.when(k > 0)
-                    def _():
-                        pl.semaphore_wait(z_free.at[way, j], 1)
-
-                    z_copy(k, j, way).start()
-
-            else:
+                    z_copy(k - 1, n, way).wait_send()
+
+                fill(last - n + z if way == 0 else n - last + z)
+
+                @pl.when(k > 0)
+                def _():
+                    pl.semaphore_wait(z_free.at[way, n], 1)
+
+                z_copy(k, n, way).start()
+
+            if j < 2:
+
+                @pl.when(near == 0)
+                def _():
+                    for n in range(2) if j == 0 else range(2, planes - 1):
+
+                        def fill(dest):
+                            zsend[way, n] = zo[:, dest]
+
+                        if n <= planes - 2:
+                            put(n, fill)
+
+            if 1 <= j <= planes - 2:
+
+                @pl.when((near >= 1) & (near <= j))
+                def _():
+                    def fill(dest):
+                        z_copy(k, j - 1, way).wait_recv()
+
+                        def add(i, carry):
+                            t, e = i // halves, i % halves
+                            value = zo[t, dest, e].astype(F32) + zrecv[way, j - 1, t, e].astype(F32)
+                            zsend[way, j, t, e] = value.astype(BF16)
+                            return carry
+
+                        lax.fori_loop(0, towers * halves, add, 0)
+                        freed()
+
+                    put(j, fill)
+
+            if j == planes - 1:
 
                 @pl.when(near >= 1)
                 def _():
@@ -639,7 +644,7 @@
 
     ready = per_chunk - 1 + 5
     offsets = [2 + 3 * j for j in range(planes)]
-    ends = [2 + 10 * j for j in range(planes)]
+    ends = [2 + 11 * j - j // 3 for j in range(planes)]
     first = per_chunk + 3
     late = (chunks - 1) * per_chunk + 3
 

time: 423 us -> 424 us (level)
  no operation moved by 1% of the time
where the time goes in v8:
time: 424 us; the launch traced here: 423 us
  Pallas kernels  421 us (99%)
    pallas_call x1, Pallas kernels, fused(): pl.pallas_call(functools.partial(kernel, planes), out_shape=(jax.ShapeDty...  405 us
    pallas_call x1, Pallas kernels, results(): pl.pallas_call(put_out, grid=(steps,), out_shape=(*(jax.ShapeDtypeStruct(...  15.3 us

profile of v8, /device:TPU:8, one launch (start us, length us, event | category | flops | bytes accessed | tf_op | source)
XLA Modules:
  0.0 423.3 jit_solution(4790719615046015028)
XLA Ops:
  0.6 405.5 %towers.1 = (bf16[2,8,64,2048]{3,2,1,0:T(8,128)(2,1)}, bf16[2,2048,1152]{2,1,0:T(8,128)(2,1)}, f32[2,2,8,64,1152]{4,3,2,1,0:T(8,128)}, f32[2,512]{1,0:T(2,128)},...) custom-call(bf16[2,2048,1152]{2,1,0:T(8,128)(2,1)} %x_hbm.1, ...), custom_call_target="tpu_custom_call" | custom-call | tf_op jit(solution)/shard_map/towers/pallas_call | solution.py:805
  406.1 0.0 copy-start.2
  406.1 0.0 copy-start.1
  406.2 0.0 copy-start
  406.2 15.3 %results.1 = (bf16[1024,2048]{1,0:T(8,128)(2,1)}, bf16[4096,1152]{1,0:T(8,128)(2,1)}, f32[2,1152,1024]{2,1,0:T(8,128)}) custom-call(bf16[1024,2048]{1,0:T(8,128)(2,1)} %bitcast.11, bf16[4096,1152]{1,0:T(8,128)(2,1)} %bitcast.8, f32[2,1024,1152]{2,1,0:T(8,128)} %bitcast.9), custom_call_target="tpu_custom_call" | custom-call | tf_op jit(solution)/shard_map/results/pallas_call | solution.py:777
  421.5 0.0 copy-done.2
  421.5 0.6 slice_reduce_fusion
  422.1 0.0 copy-done.1
  422.1 0.6 copy.16
  422.7 0.0 copy-done
  422.7 0.6 copy.17
Async XLA Ops:
  406.1 15.4 %copy-start.2 = (f32[8,128]{1,0:T(8,128)S(1)}, f32[8,128]{1,0:T(8,128)}, u32[]{:S(2)}) copy-start(f32[8,128]{1,0:T(8,128)} %get-tuple-element.23) | copy-start | bytes 12292
  406.1 16.0 %copy-start.1 = (f32[2,512]{1,0:T(2,128)S(1)}, f32[2,512]{1,0:T(2,128)}, u32[]{:S(2)}) copy-start(f32[2,512]{1,0:T(2,128)} %get-tuple-element.33) | copy-start | bytes 12292
  406.2 16.6 %copy-start = (f32[2,2,512]{2,1,0:T(2,128)S(1)}, f32[2,2,512]{2,1,0:T(2,128)}, u32[]{:S(2)}) copy-start(f32[2,2,512]{2,1,0:T(2,128)} %get-tuple-element.34) | copy-start | bytes 24580
